TPU v7x, 32 devices: a whole 2x2x4 slice. The times are simulated.
32 devices in a mesh: group: 2 (over y), context: 4 (over z), head: 4 (over x, core).
Axes of the slice: x: 2, y: 2, z: 4, core: 2. Of those that a mesh axis runs over, the one named last changes fastest.
Arguments:
- dn_query: bfloat16 [1024, 2048], P(('group', 'context'), 'head'), parts along dimension 0, may hold values from -6 to 6
- dn_key: bfloat16 [1024, 2048], P(('group', 'context'), 'head'), parts along dimension 0, may hold values from -6 to 6
- dn_value: bfloat16 [1024, 4096], P(('group', 'context'), 'head'), parts along dimension 0, may hold values from -6 to 6
- dn_gate: bfloat16 [1024, 4096], P(('group', 'context'), 'head'), parts along dimension 0, may hold values from -6 to 6
- dn_beta_logit: float32 [1024, 32], P(('group', 'context'), 'head'), parts along dimension 0, may hold values from -6 to 6
- dn_decay: float32 [1024, 32], P(('group', 'context'), 'head'), parts along dimension 0, may hold values from -1 to 0
- dn_norm_gain: float32 [128], replicated, may hold values from 0.1 to 1.9
- prefix_state: bfloat16 [4, 32, 128, 128], P('group', 'head', 'context'), parts along dimension 0, may hold values from -6 to 6
- at_query: bfloat16 [1024, 4096], P(('group', 'context'), 'head'), parts along dimension 0, may hold values from -6 to 6
- at_gate: bfloat16 [1024, 4096], P(('group', 'context'), 'head'), parts along dimension 0, may hold values from -6 to 6
- at_key: bfloat16 [1024, 512], P(('group', 'context')), parts along dimension 0, may hold values from -6 to 6
- at_value: bfloat16 [1024, 512], P(('group', 'context')), parts along dimension 0, may hold values from -6 to 6
- prefix_key: bfloat16 [16, 64, 512], P(('group', 'context')), parts along dimension 0, may hold values from -6 to 6
- prefix_value: bfloat16 [16, 64, 512], P(('group', 'context')), parts along dimension 0, may hold values from -6 to 6
- req_len: int32 [8], P('group'), parts along dimension 0, may hold values from 1 to 256, 512 in all
- req_prefix: int32 [8], P('group'), parts along dimension 0, may hold values from 0 to 1, as said below
- req_offset: int32 [8], P('group'), parts along dimension 0, may hold values from 64 to 256, as said below
- block_table: int32 [16], P('group'), parts along dimension 0, may hold values from 0 to 7, each once
Outputs:
- dn_out: bfloat16 [1024, 4096], P(('group', 'context'), 'head'), parts along dimension 0
- at_out: bfloat16 [1024, 4096], P(('group', 'context'), 'head'), parts along dimension 0
There are 2 independent parts, one for each index of `group`. A program takes and returns all parts, laid end to end along the dimension named above; an argument that names none is the same for every part. Nothing has to cross between parts.
Inputs may be any that keep to these rules, and one draw needn't show every extreme that they name: `req_len`: requests lie one after another in row order; the longest has exactly 256 new tokens. `req_prefix`: every prefix is extended by one or more requests. `req_offset`: equal for the requests of one prefix: the number of its cached positions; one prefix holds 256, another from a quarter to a half of 256. `block_table`: entry p * 4 + j is the slot of block j of prefix p; every slot once.
All inputs are finite; a program needn't handle non-finite values.
Results may differ from a plain program's by a relative error of at most 0.011.
Values may be sent and summed in bfloat16 or wider, within the bound.
A program may use at most 128 MiB of HBM per device.

v0:
```python
import math

import jax
import jax.numpy as jnp
from jax import lax
from jax.sharding import PartitionSpec as P

VH = 32
KH = 16
DK = 128
DV = 128
HQ = 16
KVH = 2
HD = 256
ROT = 64


ROPE_THETA = 10000000.0
YARN_FACTOR = 4.0
YARN_ANCHOR = 262144.0
NEG_LARGE = -1e30
HIGH = lax.Precision.HIGHEST


def carried_in(x, axis, join, neutral):
    place = lax.axis_index(axis)
    gathered = jax.tree.map(
        lambda a, kind: lax.all_gather(a.astype(kind), axis),
        x,
        (jnp.bfloat16, jnp.bfloat16, jnp.bfloat16),
    )
    state = jax.tree.map(lambda a, e: jnp.zeros_like(a) + jnp.asarray(e, a.dtype), x, neutral)

    def one(turn, state):
        return join(
            state,
            jax.tree.map(
                lambda a, own: lax.dynamic_index_in_dim(a, turn, 0, False).astype(own.dtype),
                gathered,
                x,
            ),
        )

    return lax.fori_loop(0, place, one, state)


def yarn_tables(positions, rotary):
    half = rotary // 2
    log_theta = math.log(ROPE_THETA)
    lower = max(
        math.floor(rotary * math.log(YARN_ANCHOR / (64.0 * math.pi)) / (2.0 * log_theta)), 0
    )
    upper = min(
        math.ceil(rotary * math.log(YARN_ANCHOR / (2.0 * math.pi)) / (2.0 * log_theta)), rotary - 1
    )
    spread = float(upper - lower)
    index = jnp.arange(half, dtype=jnp.float32)
    plain_frequency = jnp.exp(index * (-2.0 * log_theta / rotary))
    keep = 1.0 - jnp.clip((index - lower) / spread, 0.0, 1.0)
    frequency = plain_frequency * keep + plain_frequency / YARN_FACTOR * (1.0 - keep)
    angles = positions.astype(jnp.float32)[:, None] * frequency[None, :]
    attention_factor = 0.1 * math.log(YARN_FACTOR) + 1.0
    return (jnp.cos(angles) * attention_factor, jnp.sin(angles) * attention_factor)


def rotate(values, cosines, sines, rotary):
    half = rotary // 2
    first = values[..., :half]
    second = values[..., half:rotary]
    cosines = cosines[:, None, :]
    sines = sines[:, None, :]
    return jnp.concatenate(
        [first * cosines - second * sines, second * cosines + first * sines, values[..., rotary:]],
        axis=-1,
    )


def unit_rows(values):
    return values * lax.rsqrt(jnp.sum(values * values, axis=-1, keepdims=True) + 1e-06)


def row_layout(rows, req_len, req_prefix, req_offset):
    starts = jnp.cumsum(req_len) - req_len
    leading_found = (starts[None, :] <= rows[:, None]).astype(jnp.int32)
    segment = jnp.sum(leading_found, axis=1) - 1
    choose = (segment[:, None] == jnp.arange(req_len.shape[0], dtype=jnp.int32)[None, :]).astype(
        jnp.int32
    )
    first = jnp.sum(choose * starts[None, :], axis=1)
    prefix = jnp.sum(choose * req_prefix[None, :], axis=1)
    offset = jnp.sum(choose * req_offset[None, :], axis=1)
    return (segment, first, prefix, offset, offset + rows - first)


def absorb(state, queries, search_handles, values, visible):
    peak, total, summed = state
    scores = jnp.einsum(
        "thd,nd->thn", queries, search_handles, preferred_element_type=jnp.float32
    ) * search_handles.shape[-1] ** (-0.5)
    seen = visible[:, None, :]
    scores = jnp.where(seen, scores, NEG_LARGE)
    new_peak = jnp.maximum(peak, jnp.max(scores, axis=-1))
    weights = jnp.where(seen, jnp.exp(scores - new_peak[..., None]), 0.0)
    shrink = jnp.exp(peak - new_peak)
    total = total * shrink + jnp.sum(weights, axis=-1)
    summed = summed * shrink[..., None] + jnp.einsum(
        "thn,nd->thd", weights.astype(jnp.bfloat16), values, preferred_element_type=jnp.float32
    )
    return (new_peak, total, summed)


def compose(earlier, later):
    map_early, add_early, flag_early = earlier
    map_late, add_late, flag_late = later
    fresh = flag_late > 0.5
    joined_map = jnp.where(
        fresh, map_late, jnp.einsum("hij,hjk->hik", map_early, map_late, precision=HIGH)
    )
    joined_add = jnp.where(
        fresh, add_late, jnp.einsum("hvj,hjk->hvk", add_early, map_late, precision=HIGH) + add_late
    )
    return (joined_map, joined_add, jnp.maximum(flag_early, flag_late))


def shards(
    dn_query,
    dn_key,
    dn_value,
    dn_gate,
    dn_beta_logit,
    dn_decay,
    dn_norm_gain,
    prefix_state,
    at_query,
    at_gate,
    at_key,
    at_value,
    prefix_key,
    prefix_value,
    req_len,
    req_prefix,
    req_offset,
    block_table,
):
    tokens_here = dn_query.shape[0]
    key_heads = dn_query.shape[1] // DK
    value_heads = dn_value.shape[1] // DV
    query_heads = at_query.shape[1] // HD
    device = lax.axis_index("context")
    row_start = device * tokens_here
    rows = row_start + jnp.arange(tokens_here, dtype=jnp.int32)
    segment, first, prefix, offset, position = row_layout(rows, req_len, req_prefix, req_offset)
    query = jnp.repeat(
        unit_rows(dn_query.reshape(tokens_here, key_heads, DK).astype(jnp.float32)) * DK ** (-0.5),
        VH // KH,
        axis=1,
    )
    key = jnp.repeat(
        unit_rows(dn_key.reshape(tokens_here, key_heads, DK).astype(jnp.float32)), VH // KH, axis=1
    )
    query_heads_first = jnp.transpose(query, (1, 0, 2))
    key_heads_first = jnp.transpose(key, (1, 0, 2))
    value_heads_first = jnp.transpose(
        dn_value.reshape(tokens_here, value_heads, DV).astype(jnp.float32), (1, 0, 2)
    )
    beta = jax.nn.sigmoid(dn_beta_logit).T
    same = segment[:, None] == segment[None, :]
    causal = same & (rows[:, None] >= rows[None, :])
    strict = same & (rows[:, None] > rows[None, :])
    running = jnp.dot(causal.astype(jnp.float32), dn_decay, precision=HIGH).T
    gaps = running[:, :, None] - running[:, None, :]
    decay_mat = jnp.where(causal[None], jnp.exp(jnp.where(causal[None], gaps, 0.0)), 0.0)
    key_gram = jnp.einsum("hid,hjd->hij", key_heads_first, key_heads_first, precision=HIGH)
    query_key = jnp.einsum("hid,hjd->hij", query_heads_first, key_heads_first, precision=HIGH)
    lower_mat = jnp.where(strict[None], beta[:, :, None] * key_gram * decay_mat, 0.0)
    system = jnp.eye(tokens_here, dtype=jnp.float32)[None] + lower_mat
    start_decay = jnp.exp(running)
    solve_values = beta[:, :, None] * value_heads_first
    solve_keys = (beta * start_decay)[:, :, None] * key_heads_first
    solved = jax.scipy.linalg.solve_triangular(
        system, jnp.concatenate([solve_values, solve_keys], axis=2), lower=True, unit_diagonal=True
    )
    update = solved[:, :, :DV]
    wy_keys = solved[:, :, DV:]
    mixing = decay_mat * query_key
    local_out = jnp.einsum("hij,hjv->hiv", mixing, update, precision=HIGH)
    reach = start_decay[:, :, None] * query_heads_first - jnp.einsum(
        "hij,hjk->hik", mixing, wy_keys, precision=HIGH
    )
    tail = segment == segment[tokens_here - 1]
    end_gaps = running[:, tokens_here - 1 : tokens_here] - running
    end_weight = jnp.where(tail[None, :], jnp.exp(jnp.where(tail[None, :], end_gaps, 0.0)), 0.0)
    end_decay = start_decay[:, tokens_here - 1]
    identity_mat = jnp.eye(DK, dtype=jnp.float32)
    carry_map = end_decay[:, None, None] * identity_mat[None] - jnp.einsum(
        "hjk,hj,hjl->hkl", wy_keys, end_weight, key_heads_first, precision=HIGH
    )
    carry_add = jnp.einsum("hjv,hj,hjl->hvl", update, end_weight, key_heads_first, precision=HIGH)
    restart = (first[tokens_here - 1] >= row_start).astype(jnp.float32)
    identity = (
        jnp.broadcast_to(identity_mat, (value_heads, DK, DK)),
        jnp.zeros((value_heads, DV, DK), jnp.float32),
        jnp.zeros((), jnp.float32),
    )
    into_map, into_add, into_flag = carried_in(
        (carry_map, carry_add, restart), "context", compose, identity
    )
    carried = ((segment == segment[0]) & (first[0] < row_start))[None, :, None]
    through = jnp.einsum("hkl,hil->hik", into_map, reach, precision=HIGH)
    extra = jnp.einsum("hvk,hik->hiv", into_add, reach, precision=HIGH)
    weight_vec = jnp.where(carried, through, reach).astype(jnp.bfloat16)
    core = local_out + jnp.where(carried, extra, 0.0)
    owner_ids = jnp.arange(prefix_state.shape[0], dtype=jnp.int32)
    select = (prefix[None, :] == owner_ids[:, None]).astype(jnp.bfloat16)
    masked = select[:, None, :, None] * weight_vec[None]
    state_part = jnp.einsum(
        "phik,phvk->hiv",
        masked,
        lax.all_gather(prefix_state, "context", axis=2, tiled=True),
        preferred_element_type=jnp.float32,
    )
    core = core + state_part
    core_rows = jnp.transpose(core, (1, 0, 2))
    normed = core_rows * lax.rsqrt(jnp.mean(core_rows * core_rows, axis=-1, keepdims=True) + 1e-06)
    gate_rows = dn_gate.reshape(tokens_here, value_heads, DV).astype(jnp.float32)
    dn_out = (
        (normed * dn_norm_gain * jax.nn.silu(gate_rows))
        .reshape(tokens_here, value_heads * DV)
        .astype(jnp.bfloat16)
    )
    group = HQ // KVH
    kv_head = lax.axis_index("head") * query_heads // group
    cosines, sines = yarn_tables(position, ROT)
    query_rot = rotate(
        at_query.reshape(tokens_here, query_heads, HD).astype(jnp.float32), cosines, sines, ROT
    ).astype(jnp.bfloat16)
    new_key = lax.dynamic_slice_in_dim(at_key, kv_head * HD, HD, 1).reshape(tokens_here, 1, HD)
    new_key = (
        rotate(new_key.astype(jnp.float32), cosines, sines, ROT)
        .reshape(tokens_here, HD)
        .astype(jnp.bfloat16)
    )
    new_value = lax.dynamic_slice_in_dim(at_value, kv_head * HD, HD, 1)
    cached_key = lax.dynamic_slice_in_dim(prefix_key, kv_head * HD, HD, 2)
    cached_value = lax.dynamic_slice_in_dim(prefix_value, kv_head * HD, HD, 2)
    table_index = jnp.arange(block_table.shape[0], dtype=jnp.int32)
    blocks_per_prefix = block_table.shape[0] // prefix_state.shape[0]
    state = (
        jnp.full((tokens_here, query_heads), NEG_LARGE, jnp.float32),
        jnp.zeros((tokens_here, query_heads), jnp.float32),
        jnp.zeros((tokens_here, query_heads, HD), jnp.float32),
    )
    search_handles = lax.all_gather(cached_key, "context", axis=0, tiled=True)
    values = lax.all_gather(cached_value, "context", axis=0, tiled=True)
    count = search_handles.shape[0]
    width = search_handles.shape[1]
    slots = jnp.arange(count, dtype=jnp.int32)
    entry = jnp.sum(
        jnp.where(block_table[None, :] == slots[:, None], table_index[None, :], 0), axis=1
    )
    owner = jnp.repeat(entry // blocks_per_prefix, width)
    where_in = (
        (entry % blocks_per_prefix)[:, None] * width + jnp.arange(width, dtype=jnp.int32)[None, :]
    ).reshape(count * width)
    visible = (owner[None, :] == prefix[:, None]) & (where_in[None, :] < offset[:, None])
    flat_keys = search_handles.reshape(count * width, search_handles.shape[2])
    flat_values = values.reshape(count * width, values.shape[2])
    state = absorb(state, query_rot, flat_keys, flat_values, visible)
    search_handles = lax.all_gather(new_key, "context", axis=0, tiled=True)
    values = lax.all_gather(new_value, "context", axis=0, tiled=True)
    key_rows = jnp.arange(search_handles.shape[0], dtype=jnp.int32)
    key_segment = row_layout(key_rows, req_len, req_prefix, req_offset)[0]
    visible = (key_segment[None, :] == segment[:, None]) & (key_rows[None, :] <= rows[:, None])
    state = absorb(state, query_rot, search_handles, values, visible)
    peak, total, summed = state
    attention = summed / total[..., None]
    gate_att = at_gate.reshape(tokens_here, query_heads, HD).astype(jnp.float32)
    at_out = (
        (attention * jax.nn.sigmoid(gate_att))
        .reshape(tokens_here, query_heads * HD)
        .astype(jnp.bfloat16)
    )
    return (dn_out, at_out)


def solution(mesh):
    placed = (
        P(("group", "context"), "head"),
        P(("group", "context"), "head"),
        P(("group", "context"), "head"),
        P(("group", "context"), "head"),
        P(("group", "context"), "head"),
        P(("group", "context"), "head"),
        P(),
        P("group", "head", "context", None),
        P(("group", "context"), "head"),
        P(("group", "context"), "head"),
        P(("group", "context"), None),
        P(("group", "context"), None),
        P(("group", "context"), None, None),
        P(("group", "context"), None, None),
        P("group"),
        P("group"),
        P("group"),
        P("group"),
    )
    return jax.shard_map(
        shards,
        mesh=mesh,
        in_specs=placed,
        out_specs=(P(("group", "context"), "head"), P(("group", "context"), "head")),
        check_vma=False,
    )
```

profile of v0, /device:TPU:28, one launch (start us, length us, event | category | flops | bytes accessed | tf_op | source)
XLA Modules:
  0.0 243.2 jit_solution(15976261732324481945)
XLA Ops:
  7.3 0.7 copy-done.35
  8.3 0.7 fusion.73
  9.1 0.7 fusion.74
  11.4 0.6 copy-done.25
  12.8 2.1 fusion.15
  14.9 79.4 %custom-call.4 = f32[8,1,128,128]{2,3,1,0:T(8,128)S(1)} custom-call(f32[8,1,128,128]{3,2,1,0:T(8,128)} %fusion.15), custom_call_target="InvertDiagBlocksLowerTriangular" | custom-call | tf_op jit(solution)/shard_map/jit(_solve_triangular)/vmap()/triangular_solve | solution.py:180
  94.3 1.8 compare_and_fusion.3
  96.7 1.0 fusion.22
  97.8 1.7 convolution_convert_fusion
  99.8 1.7 fusion.20
  101.6 0.8 copy-done.11
  102.8 0.8 slice.68
  104.2 16.6 %all-gather.2 = bf16[512,1,256]{0,2,1:T(8,128)(2,1)} all-gather(bf16[128,1,256]{0,2,1:T(8,128)(2,1)S(1)} %pad_maximum_fusion.1), channel_id=4, replica_groups=mesh['group'=2,'context'=4,'head'=4] {'context'}, dimensions={0}, use_global_device_ids=true | all-gather | bytes 327680 | tf_op jit(solution)/shard_map/all_gather | solution.py:269
  121.0 0.7 fusion.49
  121.7 16.6 %all_gather.40 = bf16[8,64,256]{2,1,0:T(8,128)(2,1)} all-gather(bf16[2,64,256]{2,1,0:T(8,128)(2,1)S(1)} %constant_dynamic-slice_fusion.3), channel_id=1, replica_groups=mesh['group'=2,'context'=4,'head'=4] {'context'}, dimensions={0}, use_global_device_ids=true | all-gather | bytes 327680 | tf_op jit(solution)/shard_map/all_gather | solution.py:253
  138.8 16.8 %all_gather.41 = bf16[8,64,256]{2,1,0:T(8,128)(2,1)} all-gather(bf16[2,64,256]{2,1,0:T(8,128)(2,1)S(1)} %constant_dynamic-slice_fusion.2), channel_id=1, replica_groups=mesh['group'=2,'context'=4,'head'=4] {'context'}, dimensions={0}, use_global_device_ids=true | all-gather | bytes 327680 | tf_op jit(solution)/shard_map/all_gather | solution.py:254
  155.5 16.4 %all_gather.43 = bf16[512,256]{1,0:T(8,128)(2,1)} all-gather(bf16[128,256]{1,0:T(8,128)(2,1)S(1)} %constant_dynamic-slice_fusion.4), channel_id=1, replica_groups=mesh['group'=2,'context'=4,'head'=4] {'context'}, dimensions={0}, use_global_device_ids=true | all-gather | bytes 327680 | tf_op jit(solution)/shard_map/all_gather | solution.py:270
  172.3 1.0 copy.164
  173.4 0.8 multiply_reduce_fusion.2
  175.3 0.6 copy-done.5
  178.0 0.7 fusion.26
  179.3 0.6 dynamic-slice
  179.9 1.2 fusion.18
  181.6 1.9 dynamic-update-slice
  183.5 2.3 fusion.19
  185.8 0.6 copy-done.39
  186.4 8.7 %all-reduce = bf16[4]{0:T(256)(128)(2,1)} all-reduce(bf16[4]{0:T(256)(128)(2,1)S(1)} %copy-done.39), channel_id=1, replica_groups=mesh['group'=2,'context'=4,'head'=4] {'context'}, use_global_device_ids=true, to_apply=%add | all-reduce | flops 4 | bytes 16
  195.2 1.1 copy.165
  196.3 0.9 copy.167
  197.4 0.9 copy-done.17
  198.3 0.9 copy-done.13
  199.6 15.1 %all_gather.39 = bf16[2,8,128,128]{3,2,0,1:T(8,128)(2,1)S(1)} all-gather(bf16[2,8,32,128]{3,2,0,1:T(8,128)(2,1)S(1)} %copy.150), channel_id=1, replica_groups=mesh['group'=2,'context'=4,'head'=4] {'context'}, dimensions={2}, use_global_device_ids=true | all-gather | bytes 655360 | tf_op jit(solution)/shard_map/all_gather | solution.py:219
  215.3 0.6 copy-done.19
  216.0 1.2 convolution_multiply_fusion.3
  217.2 1.5 fusion.43
  218.7 0.7 convolution_subtract_fusion.1
  220.0 11.2 %while.14 = (s32[]{:T(128)}, f32[8,128,128]{1,2,0:T(8,128)S(1)}, f32[8,128,128]{1,2,0:T(8,128)S(1)}, s32[]{:T(128)}, bf16[4]{0:T(256)(128)(2,1)S(1)}, /*index=5*...) while((s32[]{:T(128)}, f32[8,128,128]{1,2,0:T(8,128)S(1)}, ...), condition=%wide.region_6.7_spmd, body=%wide.region_5.6_spmd.sunk | while | flops 403308544 | bytes 7340196 | solution.py:44
  220.0 1.1 constant_dynamic-slice_fusion.7
  221.3 0.6 dynamic_slice.39
  223.8 1.1 constant_dynamic-slice_fusion.7
  225.0 0.6 dynamic_slice.39
  227.5 1.1 constant_dynamic-slice_fusion.7
  228.8 0.6 dynamic_slice.39
  231.9 0.7 fusion.21
  232.9 0.7 copy-done.1
  233.6 0.8 multiply_reduce_fusion
  234.4 0.6 copy-done.30
  235.5 0.9 copy.166
  (167 shorter events, 15.8 us)
Async XLA Ops:
  7.2 96.5 %copy-start = (bf16[128,512]{1,0:T(8,128)(2,1)S(1)}, bf16[128,512]{1,0:T(8,128)(2,1)}, u32[]{:S(2)}) copy-start(bf16[128,512]{1,0:T(8,128)(2,1)} %param.30) | copy-start | bytes 393220
  7.2 212.2 %all-gather.8.cloned.1.call-start = ((), (), s32[]{:S(2)}) async-start(), calls=%async_computation.1 | async-start | bytes 1310720 | tf_op jit(solution)/shard_map/all_gather | solution.py:28
  7.2 3.6 %copy-start.15 = (bf16[128,512]{1,0:T(8,128)(2,1)S(1)}, bf16[128,512]{1,0:T(8,128)(2,1)}, u32[]{:S(2)}) copy-start(bf16[128,512]{1,0:T(8,128)(2,1)} %param.21) | copy-start | bytes 393220
  7.3 92.5 %copy-start.2 = (f32[128,128]{1,0:T(8,128)}, f32[128,128]{1,0:T(8,128)S(1)}, u32[]{:S(2)}) copy-start(f32[128,128]{1,0:T(8,128)S(1)} %get-tuple-element.158) | copy-start | bytes 196612
  7.3 0.7 copy-start.35
  8.3 0.7 copy-start.32
  8.3 0.7 copy-start.33
  9.0 166.1 %copy-start.28 = (s32[128]{0:T(128)}, s32[128]{0:T(128)S(1)}, u32[]{:S(2)}) copy-start(s32[128]{0:T(128)S(1)} %get-tuple-element.108) | copy-start | bytes 1540
  9.0 1.3 copy-start.34
  10.6 85.6 %copy-start.18 = (f32[8,128]{1,0:T(8,128)}, f32[8,128]{1,0:T(8,128)S(1)}, u32[]{:S(2)}) copy-start(f32[8,128]{1,0:T(8,128)S(1)} %convolution_bitcast_fusion.3) | copy-start | bytes 12292
  11.4 0.7 copy-start.25
  11.4 1.0 copy-start.10
  96.2 3.4 %copy-start.20 = (f32[8,128]{1,0:T(8,128)}, f32[8,128]{1,0:T(8,128)S(1)}, u32[]{:S(2)}) copy-start(f32[8,128]{1,0:T(8,128)S(1)} %get-tuple-element.135) | copy-start | bytes 12292
  99.5 119.8 %all-gather.6.cloned.1.call-start = ((), (), s32[]{:S(2)}) async-start(), calls=%async_computation | async-start | bytes 1310720 | tf_op jit(solution)/shard_map/all_gather | solution.py:28
  101.5 0.9 copy-start.11
  120.8 1.0 copy-start.22
  121.7 16.6 %copy-start.36 = (s32[8]{0:T(128)S(1)}, s32[8]{0:T(128)}, u32[]{:S(2)}) copy-start(s32[8]{0:T(128)} %param.37) | copy-start | bytes 100
  121.7 17.0 %copy-start.23 = (bf16[2,64,512]{2,1,0:T(8,128)(2,1)S(1)}, bf16[2,64,512]{2,1,0:T(8,128)(2,1)}, u32[]{:S(2)}) copy-start(bf16[2,64,512]{2,1,0:T(8,128)(2,1)} %param.33) | copy-start | bytes 393220
  138.7 16.8 %copy-start.24 = (bf16[128,512]{1,0:T(8,128)(2,1)S(1)}, bf16[128,512]{1,0:T(8,128)(2,1)}, u32[]{:S(2)}) copy-start(bf16[128,512]{1,0:T(8,128)(2,1)} %param.31) | copy-start | bytes 393220
  155.5 16.5 %copy-start.12 = (bf16[128,1024]{1,0:T(8,128)(2,1)S(1)}, bf16[128,1024]{1,0:T(8,128)(2,1)}, u32[]{:S(2)}) copy-start(bf16[128,1024]{1,0:T(8,128)(2,1)} %param.29) | copy-start | bytes 786436
  172.3 1.0 copy-start.16
  174.9 1.0 copy-start.5
  175.0 1.0 copy-start.14
  175.1 0.9 copy-start.8
  176.0 0.9 copy-start.7
  177.4 0.6 copy-start.26
  178.0 1.9 copy-start.6
  178.7 0.7 copy-start.37
  179.9 3.6 %copy-start.4 = (f32[128,4,256]{2,0,1:T(8,128)S(1)}, f32[128,4,256]{2,0,1:T(8,128)}, u32[]{:S(2)}) copy-start(f32[128,4,256]{2,0,1:T(8,128)} %copy.164) | copy-start | bytes 1572868
  183.5 2.3 copy-start.9
  185.8 0.6 copy-start.39
  185.8 9.3 %copy-start.3 = (f32[128,128]{1,0:T(8,128)S(1)}, f32[128,128]{1,0:T(8,128)}, u32[]{:S(2)}) copy-start(f32[128,128]{1,0:T(8,128)} %copy-done.2) | copy-start | bytes 196612
  197.4 0.9 copy-start.17
  198.3 0.9 copy-start.13
  199.6 15.2 %copy-start.29 = (s32[128]{0:T(128)S(1)}, s32[128]{0:T(128)}, u32[]{:S(2)}) copy-start(s32[128]{0:T(128)} %copy-done.28) | copy-start | bytes 1540
  215.3 0.7 copy-start.19
  217.2 1.5 copy-start.21
  219.4 0.6 copy-start.38
  231.3 0.6 copy-start.27
  231.9 0.7 copy-start.31
  232.5 1.0 copy-start.1
  234.4 0.7 copy-start.30
Sparse Core Ops, SparseCore 0:
  99.7 33.4 all-gather.7
  135.3 32.5 all-gather.5
where the time goes:
time: 244 us; the launch traced here: 243 us
  blocking collectives  90.2 us (37%)
  other arithmetic  87.6 us (36%)
  local copies, waits for them, and re-layouts  27.8 us (11%)
  matrix products  19.2 us (8%)
  between operations  16.1 us (7%)
    another operation x2, other arithmetic, shards(): jax.scipy.linalg.solve_triangular(system, jnp.concatenate([solve_values,...  79.4 us
    all_gather x1, blocking collectives, shards(): values = lax.all_gather(cached_value, 'context', axis=0, tiled=True)  16.8 us
    all_gather x1, blocking collectives, shards(): search_handles = lax.all_gather(new_key, 'context', axis=0, tiled=True)  16.6 us
    all_gather x1, blocking collectives, shards(): search_handles = lax.all_gather(cached_key, 'context', axis=0, tiled=True)  16.6 us
    all_gather x1, blocking collectives, shards(): values = lax.all_gather(new_value, 'context', axis=0, tiled=True)  16.4 us
    unnamed x91, local copies, waits for them, and re-layouts  15.3 us
    all_gather x1, blocking collectives, shards(): lax.all_gather(prefix_state, 'context', axis=2, tiled=True)  15.1 us
    unnamed x1, blocking collectives  8.68 us
  transfers between devices with their start and end apart: 2, of which 0 were waited for; matrix products, arithmetic and copies ran while one was open for 9% of the time, Pallas kernels for 0%

commit v1 on v0

--- a/solution.py
+++ b/solution.py
@@ -3,6 +3,8 @@
 import jax
 import jax.numpy as jnp
 from jax import lax
+from jax.experimental import pallas as pl
+from jax.experimental.pallas import tpu as pltpu
 from jax.sharding import PartitionSpec as P
 
 VH = 32
@@ -22,26 +24,91 @@
 HIGH = lax.Precision.HIGHEST
 
 
-def carried_in(x, axis, join, neutral):
-    place = lax.axis_index(axis)
-    gathered = jax.tree.map(
-        lambda a, kind: lax.all_gather(a.astype(kind), axis),
-        x,
-        (jnp.bfloat16, jnp.bfloat16, jnp.bfloat16),
-    )
-    state = jax.tree.map(lambda a, e: jnp.zeros_like(a) + jnp.asarray(e, a.dtype), x, neutral)
-
-    def one(turn, state):
-        return join(
-            state,
-            jax.tree.map(
-                lambda a, own: lax.dynamic_index_in_dim(a, turn, 0, False).astype(own.dtype),
-                gathered,
-                x,
-            ),
+def exchange_kernel(count, size, later_only, *refs):
+    sources, targets = refs[:count], refs[count : 2 * count]
+    send_sem, recv_sem, own_sem = refs[2 * count :]
+    me = lax.axis_index("context")
+    barrier = pltpu.get_barrier_semaphore()
+    for step in range(1, size):
+        pl.semaphore_signal(barrier, inc=1, device_id={"context": lax.rem(me + step, size)})
+    pl.semaphore_wait(barrier, size - 1)
+
+    def sent(step, which):
+        return pltpu.make_async_remote_copy(
+            src_ref=sources[which],
+            dst_ref=targets[which].at[me],
+            send_sem=send_sem.at[which, step - 1],
+            recv_sem=recv_sem.at[which, step - 1],
+            device_id={"context": lax.rem(me + step, size)},
         )
 
-    return lax.fori_loop(0, place, one, state)
+    own = [
+        pltpu.make_async_copy(sources[which], targets[which].at[me], own_sem.at[which])
+        for which in range(count)
+    ]
+    for step in range(1, size):
+
+        def begin(step=step):
+            for which in range(count):
+                sent(step, which).start()
+
+        if later_only:
+            pl.when(me + step < size)(begin)
+        else:
+            begin()
+    for copy in own:
+        copy.start()
+    for step in range(1, size):
+
+        def end_send(step=step):
+            for which in range(count):
+                sent(step, which).wait_send()
+
+        def end_recv(step=step):
+            for which in range(count):
+                sent(step, which).wait_recv()
+
+        if later_only:
+            pl.when(me + step < size)(end_send)
+            pl.when(me >= step)(end_recv)
+        else:
+            end_send()
+            end_recv()
+    for copy in own:
+        copy.wait()
+
+
+def exchange(arrays, size, number, later_only=False):
+    count = len(arrays)
+    return pl.pallas_call(
+        lambda *refs: exchange_kernel(count, size, later_only, *refs),
+        out_shape=[jax.ShapeDtypeStruct((size,) + a.shape, a.dtype) for a in arrays],
+        in_specs=[pl.BlockSpec(memory_space=pl.ANY)] * count,
+        out_specs=[pl.BlockSpec(memory_space=pl.ANY)] * count,
+        scratch_shapes=[
+            pltpu.SemaphoreType.DMA((count, size - 1)),
+            pltpu.SemaphoreType.DMA((count, size - 1)),
+            pltpu.SemaphoreType.DMA((count,)),
+        ],
+        compiler_params=pltpu.CompilerParams(collective_id=number, has_side_effects=True),
+    )(*arrays)
+
+
+def unit_lower_inverse(lower):
+    size = lower.shape[-1]
+    index = jnp.arange(size)
+    inverse = jnp.eye(size, dtype=jnp.float32)[None] - jnp.where(
+        (index[:, None] // 2 == index[None, :] // 2)[None], lower, 0.0
+    )
+    width = 2
+    while width < size:
+        block = index // width
+        pair = (block[:, None] // 2 == block[None, :] // 2) & (block[:, None] > block[None, :])
+        cross = jnp.where(pair[None], lower, 0.0)
+        half = jnp.einsum("hij,hjk->hik", cross, inverse, precision=HIGH)
+        inverse = inverse - jnp.einsum("hij,hjk->hik", inverse, half, precision=HIGH)
+        width *= 2
+    return inverse
 
 
 def yarn_tables(positions, rotary):
@@ -107,19 +174,6 @@
         "thn,nd->thd", weights.astype(jnp.bfloat16), values, preferred_element_type=jnp.float32
     )
     return (new_peak, total, summed)
-
-
-def compose(earlier, later):
-    map_early, add_early, flag_early = earlier
-    map_late, add_late, flag_late = later
-    fresh = flag_late > 0.5
-    joined_map = jnp.where(
-        fresh, map_late, jnp.einsum("hij,hjk->hik", map_early, map_late, precision=HIGH)
-    )
-    joined_add = jnp.where(
-        fresh, add_late, jnp.einsum("hvj,hjk->hvk", add_early, map_late, precision=HIGH) + add_late
-    )
-    return (joined_map, joined_add, jnp.maximum(flag_early, flag_late))
 
 
 def shards(
@@ -150,6 +204,28 @@
     row_start = device * tokens_here
     rows = row_start + jnp.arange(tokens_here, dtype=jnp.int32)
     segment, first, prefix, offset, position = row_layout(rows, req_len, req_prefix, req_offset)
+    size = lax.axis_size("context")
+    query_heads_here = query_heads
+    kv_head = lax.axis_index("head") * query_heads_here // (HQ // KVH)
+    cosines, sines = yarn_tables(position, ROT)
+    new_key = lax.dynamic_slice_in_dim(at_key, kv_head * HD, HD, 1).reshape(tokens_here, 1, HD)
+    new_key = (
+        rotate(new_key.astype(jnp.float32), cosines, sines, ROT)
+        .reshape(tokens_here, HD)
+        .astype(jnp.bfloat16)
+    )
+    new_value = lax.dynamic_slice_in_dim(at_value, kv_head * HD, HD, 1)
+    cached_key = lax.dynamic_slice_in_dim(prefix_key, kv_head * HD, HD, 2)
+    cached_value = lax.dynamic_slice_in_dim(prefix_value, kv_head * HD, HD, 2)
+    states, old_keys, old_values, new_keys, new_values = exchange(
+        [prefix_state, cached_key, cached_value, new_key, new_value], size, 0
+    )
+    states = jnp.moveaxis(states, 0, 2)
+    states = states.reshape(states.shape[:2] + (-1, DK))
+    old_keys = old_keys.reshape((-1,) + old_keys.shape[2:])
+    old_values = old_values.reshape((-1,) + old_values.shape[2:])
+    new_keys = new_keys.reshape(-1, HD)
+    new_values = new_values.reshape(-1, HD)
     query = jnp.repeat(
         unit_rows(dn_query.reshape(tokens_here, key_heads, DK).astype(jnp.float32)) * DK ** (-0.5),
         VH // KH,
@@ -173,12 +249,14 @@
     key_gram = jnp.einsum("hid,hjd->hij", key_heads_first, key_heads_first, precision=HIGH)
     query_key = jnp.einsum("hid,hjd->hij", query_heads_first, key_heads_first, precision=HIGH)
     lower_mat = jnp.where(strict[None], beta[:, :, None] * key_gram * decay_mat, 0.0)
-    system = jnp.eye(tokens_here, dtype=jnp.float32)[None] + lower_mat
     start_decay = jnp.exp(running)
     solve_values = beta[:, :, None] * value_heads_first
     solve_keys = (beta * start_decay)[:, :, None] * key_heads_first
-    solved = jax.scipy.linalg.solve_triangular(
-        system, jnp.concatenate([solve_values, solve_keys], axis=2), lower=True, unit_diagonal=True
+    solved = jnp.einsum(
+        "hij,hjk->hik",
+        unit_lower_inverse(lower_mat),
+        jnp.concatenate([solve_values, solve_keys], axis=2),
+        precision=HIGH,
     )
     update = solved[:, :, :DV]
     wy_keys = solved[:, :, DV:]
@@ -196,15 +274,31 @@
         "hjk,hj,hjl->hkl", wy_keys, end_weight, key_heads_first, precision=HIGH
     )
     carry_add = jnp.einsum("hjv,hj,hjl->hvl", update, end_weight, key_heads_first, precision=HIGH)
-    restart = (first[tokens_here - 1] >= row_start).astype(jnp.float32)
-    identity = (
-        jnp.broadcast_to(identity_mat, (value_heads, DK, DK)),
-        jnp.zeros((value_heads, DV, DK), jnp.float32),
-        jnp.zeros((), jnp.float32),
-    )
-    into_map, into_add, into_flag = carried_in(
-        (carry_map, carry_add, restart), "context", compose, identity
-    )
+    map_all, add_all = exchange(
+        [carry_map.astype(jnp.bfloat16), carry_add.astype(jnp.bfloat16)], size, 1, True
+    )
+    starts = jnp.cumsum(req_len) - req_len
+    into_map = jnp.broadcast_to(identity_mat, (value_heads, DK, DK))
+    into_add = jnp.zeros((value_heads, DV, DK), jnp.float32)
+    for turn in range(size - 1):
+        low, high = turn * tokens_here, (turn + 1) * tokens_here
+        fresh = jnp.any((starts >= low) & (starts < high))
+        used = turn < device
+        map_one = jnp.where(used, map_all[turn], 0).astype(jnp.float32)
+        add_one = jnp.where(used, add_all[turn], 0).astype(jnp.float32)
+        if turn == 0:
+            next_map, next_add = map_one, add_one
+        else:
+            both = jnp.einsum(
+                "hij,hjk->hik",
+                jnp.concatenate([into_map, into_add], axis=1),
+                map_one,
+                precision=HIGH,
+            )
+            next_map = jnp.where(fresh, map_one, both[:, :DK])
+            next_add = jnp.where(fresh, 0.0, both[:, DK:]) + add_one
+        into_map = jnp.where(used, next_map, into_map)
+        into_add = jnp.where(used, next_add, into_add)
     carried = ((segment == segment[0]) & (first[0] < row_start))[None, :, None]
     through = jnp.einsum("hkl,hil->hik", into_map, reach, precision=HIGH)
     extra = jnp.einsum("hvk,hik->hiv", into_add, reach, precision=HIGH)
@@ -216,7 +310,7 @@
     state_part = jnp.einsum(
         "phik,phvk->hiv",
         masked,
-        lax.all_gather(prefix_state, "context", axis=2, tiled=True),
+        states,
         preferred_element_type=jnp.float32,
     )
     core = core + state_part
@@ -228,21 +322,9 @@
         .reshape(tokens_here, value_heads * DV)
         .astype(jnp.bfloat16)
     )
-    group = HQ // KVH
-    kv_head = lax.axis_index("head") * query_heads // group
-    cosines, sines = yarn_tables(position, ROT)
     query_rot = rotate(
         at_query.reshape(tokens_here, query_heads, HD).astype(jnp.float32), cosines, sines, ROT
     ).astype(jnp.bfloat16)
-    new_key = lax.dynamic_slice_in_dim(at_key, kv_head * HD, HD, 1).reshape(tokens_here, 1, HD)
-    new_key = (
-        rotate(new_key.astype(jnp.float32), cosines, sines, ROT)
-        .reshape(tokens_here, HD)
-        .astype(jnp.bfloat16)
-    )
-    new_value = lax.dynamic_slice_in_dim(at_value, kv_head * HD, HD, 1)
-    cached_key = lax.dynamic_slice_in_dim(prefix_key, kv_head * HD, HD, 2)
-    cached_value = lax.dynamic_slice_in_dim(prefix_value, kv_head * HD, HD, 2)
     table_index = jnp.arange(block_table.shape[0], dtype=jnp.int32)
     blocks_per_prefix = block_table.shape[0] // prefix_state.shape[0]
     state = (
@@ -250,8 +332,8 @@
         jnp.zeros((tokens_here, query_heads), jnp.float32),
         jnp.zeros((tokens_here, query_heads, HD), jnp.float32),
     )
-    search_handles = lax.all_gather(cached_key, "context", axis=0, tiled=True)
-    values = lax.all_gather(cached_value, "context", axis=0, tiled=True)
+    search_handles = old_keys
+    values = old_values
     count = search_handles.shape[0]
     width = search_handles.shape[1]
     slots = jnp.arange(count, dtype=jnp.int32)
@@ -266,8 +348,8 @@
     flat_keys = search_handles.reshape(count * width, search_handles.shape[2])
     flat_values = values.reshape(count * width, values.shape[2])
     state = absorb(state, query_rot, flat_keys, flat_values, visible)
-    search_handles = lax.all_gather(new_key, "context", axis=0, tiled=True)
-    values = lax.all_gather(new_value, "context", axis=0, tiled=True)
+    search_handles = new_keys
+    values = new_values
     key_rows = jnp.arange(search_handles.shape[0], dtype=jnp.int32)
     key_segment = row_layout(key_rows, req_len, req_prefix, req_offset)[0]
     visible = (key_segment[None, :] == segment[:, None]) & (key_rows[None, :] <= rows[:, None])

time: 244 us -> 148 us (0.61)
  blocking collectives: 90.2 us -> 0 us
  Pallas kernels: 0 us -> 85.5 us
  other arithmetic: 87.6 us -> 15.8 us
  between operations: 16.1 us -> 1.53 us
  local copies, waits for them, and re-layouts: 27.8 us -> 19.9 us
  matrix products: 19.2 us -> 23.9 us
    pallas_call x0 -> x2, Pallas kernels: none -> 85.5 us  [exchange(): pl.pallas_call(lambda *refs: exchange_kernel(count, size, later_only, *re...]
    all_gather x5 -> x0, blocking collectives: 81.5 us -> none  [the longest x1 16.8 us: shards(): values = lax.all_gather(cached_value, 'context', axis=0, tiled=True)]
    another operation x5 -> x3, other arithmetic: 79.9 us -> 1.35 us  [the longest x2 79.4 us: shards(): jax.scipy.linalg.solve_triangular(system, jnp.concatenate([solve_values,...]
    unnamed x1 -> x0, blocking collectives: 8.68 us -> none
    dot_general x7 -> x16, matrix products: 3.15 us -> 10.7 us  [the longest x6 4.19 us: unit_lower_inverse(): half = jnp.einsum('hij,hjk->hik', cross, inverse, precision=HIGH)]
    dynamic_slice x15 -> x0, local copies, waits for them, and re-layouts: 6.16 us -> none  [the longest x12 6.04 us: one(): lax.dynamic_index_in_dim(a, turn, 0, False).astype(own.dtype)]
    select_n x0 -> x9, other arithmetic: none -> 3.04 us  [the longest x2 1.99 us: shards(): into_add = jnp.where(used, next_add, into_add)]
    dot_general x2, matrix products: 3.44 us -> 0.74 us  [absorb(): jnp.einsum('thn,nd->thd', weights.astype(jnp.bfloat16), values, preferred...]
  transfers between devices with their start and end apart: 2 -> 0, of which waited for: 0 -> 0; matrix products, arithmetic and copies ran while one was open for 9% -> 0% of each run, Pallas kernels for 0% -> 0%
where the time goes in v1:
time: 148 us; the launch traced here: 147 us
  Pallas kernels  85.5 us (58%)
  matrix products  23.9 us (16%)
  local copies, waits for them, and re-layouts  19.9 us (13%)
  other arithmetic  15.8 us (11%)
  between operations  1.53 us (1%)
    pallas_call x2, Pallas kernels, exchange(): pl.pallas_call(lambda *refs: exchange_kernel(count, size, later_only, *re...  85.5 us
    unnamed x76, local copies, waits for them, and re-layouts  13.3 us
    dot_general x6, matrix products, unit_lower_inverse(): half = jnp.einsum('hij,hjk->hik', cross, inverse, precision=HIGH)  4.19 us
    dot_general x6, matrix products, unit_lower_inverse(): jnp.einsum('hij,hjk->hik', inverse, half, precision=HIGH)  3.96 us

profile of v1, /device:TPU:28, one launch (start us, length us, event | category | flops | bytes accessed | tf_op | source)
XLA Modules:
  0.0 146.7 jit_solution(6313413307656364902)
XLA Ops:
  0.7 0.7 copy-done.33
  2.2 0.7 and_reduce_fusion.1
  4.4 1.8 %compare_and_fusion.9 = (pred[128]{0:T(512)(128)(4,1)}, pred[128]{0:T(512)(128)(4,1)S(1)}) fusion(pred[]{:T(512)S(6)} %lt.38, s32[]{:T(128)} %bitcast.11, s32[128]{0:T(128)S(1)} %convert_reduce_fusion.1, s32[]{:T(128)} %bitcast.14), kind=kLoop, calls=%fused_computation.198 | loop fusion | flops 512 | bytes 777 | tf_op jit(solution)/shard_map/and | solution.py:302
  9.4 0.7 slice_reduce_fusion.1
  10.3 0.7 compare_and_fusion.5
  11.0 0.7 compare_and_fusion.6
  11.8 0.7 compare_and_fusion.7
  12.5 0.7 broadcast_compare_fusion
  13.3 0.7 compare_and_fusion.1
  15.3 0.6 constant_dynamic-slice_fusion.1
  16.7 0.7 maximum_bitcast_fusion.refs_3_
  18.2 0.9 copy-done.9
  19.7 0.9 copy-done.3
  20.9 0.8 copy-done.4
  22.1 0.8 copy-done.5
  23.2 0.8 slice.105
  24.1 0.8 subtract_convert_fusion
  25.6 0.7 copy-done.16
  26.3 1.2 fusion.6
  27.5 1.2 convolution_multiply_fusion.3
  28.8 0.7 fusion.57
  29.5 0.7 convolution_subtract_fusion.5
  30.2 0.7 fusion.55
  30.9 0.6 convolution_subtract_fusion.4
  31.6 0.7 fusion.53
  32.3 0.6 convolution_subtract_fusion.3
  33.0 0.7 fusion.51
  33.6 0.6 convolution_subtract_fusion.2
  34.3 0.9 fusion.49
  35.2 0.6 convolution_subtract_fusion.1
  35.8 0.7 fusion.47
  36.5 0.7 convolution_subtract_fusion
  37.7 1.0 fusion.13
  38.7 0.7 convolution_subtract_fusion.7
  39.4 0.7 fusion.64
  40.1 1.7 %fusion.11.refs_0_ = bf16[8,128,128]{2,1,0:T(8,128)(2,1)} fusion(f32[8,128,128]{2,1,0:T(8,128)S(1)} %get-tuple-element.36, f32[8,128,256]{2,1,0:T(8,128)S(1)} %fusion.13, f32[8]{0:T(128)S(1)} %copy-done.23, f32[128,128]{1,0:T(8,128)S(1)} %fusion.112), kind=kOutput, calls=%fused_computation.28 | convolution fusion | flops 201719808 | bytes 1376768 | tf_op jit(solution)/shard_map/hjk,hj,hjl->hkl/dot_general | solution.py:273
  41.8 1.7 %convolution_convert_fusion.refs_1_ = bf16[8,128,128]{2,1,0:T(8,128)(2,1)} fusion(f32[8,128,128]{2,1,0:T(8,128)S(1)} %get-tuple-element.36, f32[8,128,256]{2,1,0:T(8,128)S(1)} %fusion.13), kind=kOutput, calls=%fused_computation.30 | convolution fusion | flops 201457664 | bytes 1310720 | tf_op jit(solution)/shard_map/hjv,hj,hjl->hvl/dot_general | solution.py:276
  43.6 37.7 %shard_map.186 = (bf16[4,2,8,32,128]{4,3,2,1,0:T(8,128)(2,1)}, bf16[4,2,64,256]{3,2,1,0:T(8,128)(2,1)}, bf16[4,2,64,256]{3,2,1,0:T(8,128)(2,1)}, bf16[4,128,256]{2,1,0:T(8,128)(2,1)}, bf16[4,128,256]{2,1,0:T(8,128)(2,1)}) custom-call(bf16[2,8,32,128]{3,2,1,0:T(8,128)(2,1)} %refs_0_.1, bf16[2,64,256]{2,1,0:T(8,128)(2,1)} %get-tuple-element.77.refs_1_, ...), custom_call_target="tpu_custom_call" | custom-call | tf_op jit(solution)/shard_map/pallas_call | solution.py:83
  81.3 1.2 copy.86
  86.8 0.9 copy.102
  87.7 47.8 %shard_map.185 = (bf16[4,8,128,128]{3,2,1,0:T(8,128)(2,1)}, bf16[4,8,128,128]{3,2,1,0:T(8,128)(2,1)}) custom-call(bf16[8,128,128]{2,1,0:T(8,128)(2,1)} %fusion.11.refs_0_, bf16[8,128,128]{2,1,0:T(8,128)(2,1)} %convolution_convert_fusion.refs_1_), custom_call_target="tpu_custom_call" | custom-call | tf_op jit(solution)/shard_map/pallas_call | solution.py:83
  135.6 1.1 select_bitcast_fusion
  136.7 1.0 convert_select_fusion
  138.9 0.9 fusion.37
  140.4 2.1 %fusion.12 = bf16[8,128,128]{2,1,0:T(8,128)(2,1)S(1)} fusion(f32[8,128,128]{2,1,0:T(8,128)S(1)} %convolution_subtract_fusion.7, f32[8,128,128]{2,1,0:T(8,128)S(1)} %get-tuple-element.33, f32[8,256,128]{2,1,0:T(8,128)S(1)} %fusion.21, pred[128]{0:T(512)(128)(4,1)S(1)} %copy-done.22, pred[]{:T(512)} %get-tuple-element.25, pred[]{:T(512)S(6)} %gt.137, ...), kind=kOutput, calls=%fused_computation.29 | convolution fusion | flops 202113024 | bytes 2622977 | tf_op jit(solution)/shard_map/hkl,hil->hik/dot_general | solution.py:303
  142.9 2.0 %multiply_reduce_fusion = (f32[128,8]{0,1:T(8,128)S(1)}, f32[128,8,128]{2,0,1:T(8,128)S(1)}) fusion(f32[8,128,128]{2,1,0:T(8,128)S(1)} %convolution_bitcast_fusion, f32[8,128,128]{2,1,0:T(8,128)S(1)} %fusion.64, f32[8,128,128]{2,1,0:T(8,128)S(1)} %convolution_subtract_fusion.7, f32[8,128,128]{2,1,0:T(8,128)S(1)} %get-tuple-element.32, ...), kind=kOutput, calls=%fused_computation.72 | convolution fusion | flops 202636288 | bytes 3413505 | tf_op jit(solution)/shard_map/hvk,hik->hiv/dot_general | solution.py:304
  144.8 0.6 copy-done.24
  145.9 0.9 copy.101
  (140 shorter events, 18.2 us)
Async XLA Ops:
  0.6 13.9 %copy-start = (bf16[128,512]{1,0:T(8,128)(2,1)S(1)}, bf16[128,512]{1,0:T(8,128)(2,1)}, u32[]{:S(2)}) copy-start(bf16[128,512]{1,0:T(8,128)(2,1)} %param.29) | copy-start | bytes 393220
  0.7 0.7 copy-start.33
  1.4 0.7 copy-start.25
  3.6 0.7 copy-start.26
  3.6 0.7 copy-start.27
  7.0 0.7 copy-start.32
  7.9 0.8 copy-start.21
  14.4 0.9 copy-start.17
  14.4 1.0 copy-start.18
  15.3 1.0 copy-start.19
  16.7 0.9 copy-start.8
  18.2 0.9 copy-start.9
  19.6 1.0 copy-start.3
  20.8 1.0 copy-start.4
  21.9 1.0 copy-start.5
  24.1 1.0 copy-start.6
  25.6 0.7 copy-start.16
  27.5 1.3 copy-start.15
  29.5 0.7 copy-start.14
  30.9 0.7 copy-start.13
  32.3 0.7 copy-start.12
  36.5 0.7 copy-start.20
  39.4 0.7 copy-start.23
  81.3 1.2 copy-start.7
  81.3 1.2 copy-start.10
  81.3 1.2 copy-start.11
  81.3 1.3 copy-start.31
  82.6 0.9 copy-start.30
  84.4 1.0 copy-start.29
  85.3 0.9 copy-start.28
  135.5 2.1 %copy-start.1 = (bf16[4,8,128,128]{3,2,1,0:T(8,128)(2,1)S(1)}, bf16[4,8,128,128]{3,2,1,0:T(8,128)(2,1)}, u32[]{:S(2)}) copy-start(bf16[4,8,128,128]{3,2,1,0:T(8,128)(2,1)} %get-tuple-element.9) | copy-start | bytes 3145732
  137.7 1.2 copy-start.2
  139.8 0.6 copy-start.22
  140.4 2.1 %copy-start.34 = (bf16[2,128]{1,0:T(2,128)(2,1)S(1)}, bf16[2,128]{1,0:T(2,128)(2,1)}, u32[]{:S(2)}) copy-start(bf16[2,128]{1,0:T(2,128)(2,1)} %compare_convert_fusion) | copy-start | bytes 1540
  144.8 0.7 copy-start.24

commit v2 on v1

--- a/solution.py
+++ b/solution.py
@@ -24,74 +24,73 @@
 HIGH = lax.Precision.HIGHEST
 
 
-def exchange_kernel(count, size, later_only, *refs):
-    sources, targets = refs[:count], refs[count : 2 * count]
-    send_sem, recv_sem, own_sem = refs[2 * count :]
+def chain_kernel(size, map_ref, add_ref, into_ref, held, leaving, send_sem, recv_sem):
     me = lax.axis_index("context")
+    heads = map_ref.shape[0]
     barrier = pltpu.get_barrier_semaphore()
-    for step in range(1, size):
-        pl.semaphore_signal(barrier, inc=1, device_id={"context": lax.rem(me + step, size)})
-    pl.semaphore_wait(barrier, size - 1)
-
-    def sent(step, which):
+    after, before = lax.rem(me + 1, size), lax.rem(me + size - 1, size)
+    for neighbour in (before, after):
+        pl.semaphore_signal(barrier, inc=1, device_id={"context": neighbour})
+    pl.semaphore_wait(barrier, 2)
+
+    def sent(h):
         return pltpu.make_async_remote_copy(
-            src_ref=sources[which],
-            dst_ref=targets[which].at[me],
-            send_sem=send_sem.at[which, step - 1],
-            recv_sem=recv_sem.at[which, step - 1],
-            device_id={"context": lax.rem(me + step, size)},
+            src_ref=leaving.at[h],
+            dst_ref=held.at[h],
+            send_sem=send_sem.at[h],
+            recv_sem=recv_sem.at[h],
+            device_id={"context": after},
         )
 
-    own = [
-        pltpu.make_async_copy(sources[which], targets[which].at[me], own_sem.at[which])
-        for which in range(count)
+    @pl.when(me == 0)
+    def _():
+        held[...] = jnp.zeros_like(held)
+
+    for h in range(heads):
+
+        @pl.when(me > 0)
+        def _(h=h):
+            sent(h).wait_recv()
+
+        leaving[h] = (
+            jnp.dot(held[h], map_ref[h], preferred_element_type=jnp.float32) + add_ref[h]
+        ).astype(jnp.bfloat16)
+
+        @pl.when(me < size - 1)
+        def _(h=h):
+            sent(h).start()
+
+    into_ref[...] = held[...]
+
+    @pl.when(me < size - 1)
+    def _():
+        for h in range(heads):
+            sent(h).wait_send()
+
+
+def chain(carry_map, carry_add, size):
+    heads = carry_map.shape[0]
+    return pl.pallas_call(
+        lambda *refs: chain_kernel(size, *refs),
+        out_shape=jax.ShapeDtypeStruct(carry_add.shape, jnp.bfloat16),
+        in_specs=[pl.BlockSpec(memory_space=pltpu.VMEM)] * 2,
+        out_specs=pl.BlockSpec(memory_space=pltpu.VMEM),
+        scratch_shapes=[
+            pltpu.VMEM(carry_add.shape, jnp.bfloat16),
+            pltpu.VMEM(carry_add.shape, jnp.bfloat16),
+            pltpu.SemaphoreType.DMA((heads,)),
+            pltpu.SemaphoreType.DMA((heads,)),
+        ],
+        compiler_params=pltpu.CompilerParams(collective_id=1, has_side_effects=True),
+    )(carry_map, carry_add)
+
+
+def gathered(x, size, me):
+    turned = [x] + [
+        lax.ppermute(x, "context", [(i, (i + step) % size) for i in range(size)])
+        for step in range(1, size)
     ]
-    for step in range(1, size):
-
-        def begin(step=step):
-            for which in range(count):
-                sent(step, which).start()
-
-        if later_only:
-            pl.when(me + step < size)(begin)
-        else:
-            begin()
-    for copy in own:
-        copy.start()
-    for step in range(1, size):
-
-        def end_send(step=step):
-            for which in range(count):
-                sent(step, which).wait_send()
-
-        def end_recv(step=step):
-            for which in range(count):
-                sent(step, which).wait_recv()
-
-        if later_only:
-            pl.when(me + step < size)(end_send)
-            pl.when(me >= step)(end_recv)
-        else:
-            end_send()
-            end_recv()
-    for copy in own:
-        copy.wait()
-
-
-def exchange(arrays, size, number, later_only=False):
-    count = len(arrays)
-    return pl.pallas_call(
-        lambda *refs: exchange_kernel(count, size, later_only, *refs),
-        out_shape=[jax.ShapeDtypeStruct((size,) + a.shape, a.dtype) for a in arrays],
-        in_specs=[pl.BlockSpec(memory_space=pl.ANY)] * count,
-        out_specs=[pl.BlockSpec(memory_space=pl.ANY)] * count,
-        scratch_shapes=[
-            pltpu.SemaphoreType.DMA((count, size - 1)),
-            pltpu.SemaphoreType.DMA((count, size - 1)),
-            pltpu.SemaphoreType.DMA((count,)),
-        ],
-        compiler_params=pltpu.CompilerParams(collective_id=number, has_side_effects=True),
-    )(*arrays)
+    return jnp.stack(turned), (me - jnp.arange(size, dtype=jnp.int32)) % size
 
 
 def unit_lower_inverse(lower):
@@ -217,15 +216,19 @@
     new_value = lax.dynamic_slice_in_dim(at_value, kv_head * HD, HD, 1)
     cached_key = lax.dynamic_slice_in_dim(prefix_key, kv_head * HD, HD, 2)
     cached_value = lax.dynamic_slice_in_dim(prefix_value, kv_head * HD, HD, 2)
-    states, old_keys, old_values, new_keys, new_values = exchange(
-        [prefix_state, cached_key, cached_value, new_key, new_value], size, 0
-    )
+    states, origin = gathered(prefix_state, size, device)
+    states = jnp.take(states, origin, axis=0)
     states = jnp.moveaxis(states, 0, 2)
     states = states.reshape(states.shape[:2] + (-1, DK))
-    old_keys = old_keys.reshape((-1,) + old_keys.shape[2:])
-    old_values = old_values.reshape((-1,) + old_values.shape[2:])
-    new_keys = new_keys.reshape(-1, HD)
-    new_values = new_values.reshape(-1, HD)
+    slots_here = cached_key.shape[0]
+    both, origin = gathered(
+        jnp.concatenate(
+            [cached_key.reshape(-1, HD), new_key, cached_value.reshape(-1, HD), new_value]
+        ).reshape(2, -1, HD),
+        size,
+        device,
+    )
+    cached_rows = cached_key.shape[0] * cached_key.shape[1]
     query = jnp.repeat(
         unit_rows(dn_query.reshape(tokens_here, key_heads, DK).astype(jnp.float32)) * DK ** (-0.5),
         VH // KH,
@@ -274,46 +277,32 @@
         "hjk,hj,hjl->hkl", wy_keys, end_weight, key_heads_first, precision=HIGH
     )
     carry_add = jnp.einsum("hjv,hj,hjl->hvl", update, end_weight, key_heads_first, precision=HIGH)
-    map_all, add_all = exchange(
-        [carry_map.astype(jnp.bfloat16), carry_add.astype(jnp.bfloat16)], size, 1, True
-    )
-    starts = jnp.cumsum(req_len) - req_len
-    into_map = jnp.broadcast_to(identity_mat, (value_heads, DK, DK))
-    into_add = jnp.zeros((value_heads, DV, DK), jnp.float32)
-    for turn in range(size - 1):
-        low, high = turn * tokens_here, (turn + 1) * tokens_here
-        fresh = jnp.any((starts >= low) & (starts < high))
-        used = turn < device
-        map_one = jnp.where(used, map_all[turn], 0).astype(jnp.float32)
-        add_one = jnp.where(used, add_all[turn], 0).astype(jnp.float32)
-        if turn == 0:
-            next_map, next_add = map_one, add_one
-        else:
-            both = jnp.einsum(
-                "hij,hjk->hik",
-                jnp.concatenate([into_map, into_add], axis=1),
-                map_one,
-                precision=HIGH,
-            )
-            next_map = jnp.where(fresh, map_one, both[:, :DK])
-            next_add = jnp.where(fresh, 0.0, both[:, DK:]) + add_one
-        into_map = jnp.where(used, next_map, into_map)
-        into_add = jnp.where(used, next_add, into_add)
-    carried = ((segment == segment[0]) & (first[0] < row_start))[None, :, None]
-    through = jnp.einsum("hkl,hil->hik", into_map, reach, precision=HIGH)
-    extra = jnp.einsum("hvk,hik->hiv", into_add, reach, precision=HIGH)
-    weight_vec = jnp.where(carried, through, reach).astype(jnp.bfloat16)
-    core = local_out + jnp.where(carried, extra, 0.0)
-    owner_ids = jnp.arange(prefix_state.shape[0], dtype=jnp.int32)
-    select = (prefix[None, :] == owner_ids[:, None]).astype(jnp.bfloat16)
-    masked = select[:, None, :, None] * weight_vec[None]
-    state_part = jnp.einsum(
-        "phik,phvk->hiv",
-        masked,
-        states,
-        preferred_element_type=jnp.float32,
-    )
-    core = core + state_part
+    restarts = first[tokens_here - 1] >= row_start
+    tail_prefix = prefix[tokens_here - 1]
+    base = jnp.zeros(states.shape[1:], states.dtype)
+    for owner in range(states.shape[0]):
+        base = jnp.where(tail_prefix == owner, states[owner], base)
+    map_half = carry_map.astype(jnp.bfloat16)
+    fresh = jnp.einsum("hvj,hjk->hvk", base, map_half, preferred_element_type=jnp.float32)
+    into_state = chain(
+        jnp.where(restarts, 0, map_half).astype(jnp.bfloat16),
+        carry_add + jnp.where(restarts, fresh, 0.0),
+        size,
+    )
+    carried = (segment == segment[0]) & (first[0] < row_start)
+    owner_ids = jnp.arange(states.shape[0], dtype=jnp.int32)
+    select = (prefix[None, :] == owner_ids[:, None]) & ~carried[None, :]
+    select = jnp.concatenate([select, carried[None, :]], axis=0)
+    weight_vec = reach.astype(jnp.bfloat16)
+    core = local_out
+    for owner in range(states.shape[0] + 1):
+        held = states[owner] if owner < states.shape[0] else into_state
+        core = core + jnp.einsum(
+            "hik,hvk->hiv",
+            jnp.where(select[owner][None, :, None], weight_vec, 0),
+            held,
+            preferred_element_type=jnp.float32,
+        )
     core_rows = jnp.transpose(core, (1, 0, 2))
     normed = core_rows * lax.rsqrt(jnp.mean(core_rows * core_rows, axis=-1, keepdims=True) + 1e-06)
     gate_rows = dn_gate.reshape(tokens_here, value_heads, DV).astype(jnp.float32)
@@ -332,28 +321,23 @@
         jnp.zeros((tokens_here, query_heads), jnp.float32),
         jnp.zeros((tokens_here, query_heads, HD), jnp.float32),
     )
-    search_handles = old_keys
-    values = old_values
-    count = search_handles.shape[0]
-    width = search_handles.shape[1]
-    slots = jnp.arange(count, dtype=jnp.int32)
+    part = jnp.arange(cached_rows, dtype=jnp.int32)
+    width = cached_key.shape[1]
+    slots = (origin[:, None] * slots_here + part[None, :] // width).reshape(-1)
     entry = jnp.sum(
         jnp.where(block_table[None, :] == slots[:, None], table_index[None, :], 0), axis=1
-    )
-    owner = jnp.repeat(entry // blocks_per_prefix, width)
-    where_in = (
-        (entry % blocks_per_prefix)[:, None] * width + jnp.arange(width, dtype=jnp.int32)[None, :]
-    ).reshape(count * width)
-    visible = (owner[None, :] == prefix[:, None]) & (where_in[None, :] < offset[:, None])
-    flat_keys = search_handles.reshape(count * width, search_handles.shape[2])
-    flat_values = values.reshape(count * width, values.shape[2])
-    state = absorb(state, query_rot, flat_keys, flat_values, visible)
-    search_handles = new_keys
-    values = new_values
-    key_rows = jnp.arange(search_handles.shape[0], dtype=jnp.int32)
-    key_segment = row_layout(key_rows, req_len, req_prefix, req_offset)[0]
-    visible = (key_segment[None, :] == segment[:, None]) & (key_rows[None, :] <= rows[:, None])
-    state = absorb(state, query_rot, search_handles, values, visible)
+    ).reshape(size, cached_rows)
+    owner = entry // blocks_per_prefix
+    where_in = entry % blocks_per_prefix * width + part[None, :] % width
+    key_rows = origin[:, None] * tokens_here + jnp.arange(tokens_here, dtype=jnp.int32)[None, :]
+    key_segment = row_layout(key_rows.reshape(-1), req_len, req_prefix, req_offset)[0]
+    key_segment = key_segment.reshape(size, tokens_here)
+    old_seen = (owner[None] == prefix[:, None, None]) & (where_in[None] < offset[:, None, None])
+    new_seen = (key_segment[None] == segment[:, None, None]) & (key_rows[None] <= rows[:, None, None])
+    visible = jnp.concatenate([old_seen, new_seen], axis=2).reshape(tokens_here, -1)
+    state = absorb(
+        state, query_rot, both[:, 0].reshape(-1, HD), both[:, 1].reshape(-1, HD), visible
+    )
     peak, total, summed = state
     attention = summed / total[..., None]
     gate_att = at_gate.reshape(tokens_here, query_heads, HD).astype(jnp.float32)

time: 148 us -> 94.6 us (0.64)
  Pallas kernels: 85.5 us -> 15.9 us
  starting transfers between devices: 0 us -> 8.88 us
  other arithmetic: 15.8 us -> 21 us
  between operations: 1.53 us -> 4.03 us
    pallas_call x2 -> x1, Pallas kernels: 85.5 us -> 15.9 us  [chain(): pl.pallas_call(lambda *refs: chain_kernel(size, *refs), out_shape=jax.Sha...]
    unnamed x76 -> x59, local copies, waits for them, and re-layouts: 13.3 us -> 2.53 us
    ppermute x0 -> x6, starting transfers between devices: none -> 8.88 us  [gathered(): lax.ppermute(x, 'context', [(i, (i + step) % size) for i in range(size)])]
    slice x1 -> x9, local copies, waits for them, and re-layouts: 0.58 us -> 5.39 us  [the longest x2 2.12 us: shards(): both[:, 0].reshape(-1, HD)]
    another operation x3 -> x6, other arithmetic: 1.35 us -> 5.98 us  [the longest x2 4.15 us: gathered(): return (jnp.stack(turned), (me - jnp.arange(size, dtype=jnp.int32)) % size)]
    select_n x11 -> x10, other arithmetic: 3.66 us -> 1.79 us  [the longest x1 0.62 us: shards(): owner = entry // blocks_per_prefix]
    and x5, other arithmetic: 2.31 us -> 0.51 us  [unit_lower_inverse(): (block[:, None] // 2 == block[None, :] // 2) & (block[:, None] > block[No...]
    not x0 -> x1, other arithmetic: none -> 1.78 us  [shards(): select = (prefix[None, :] == owner_ids[:, None]) & ~carried[None, :]]
  transfers between devices with their start and end apart: 0 -> 6, of which waited for: 0 -> 0; matrix products, arithmetic and copies ran while one was open for 0% -> 60% of each run, Pallas kernels for 0% -> 17%
where the time goes in v2:
time: 94.6 us; the launch traced here: 93.9 us
  matrix products  24.4 us (26%)
  other arithmetic  21 us (22%)
  local copies, waits for them, and re-layouts  19.7 us (21%)
  Pallas kernels  15.9 us (17%)
  starting transfers between devices  8.88 us (9%)
  between operations  4.03 us (4%)
    pallas_call x1, Pallas kernels, chain(): pl.pallas_call(lambda *refs: chain_kernel(size, *refs), out_shape=jax.Sha...  15.9 us
    ppermute x6, starting transfers between devices, gathered(): lax.ppermute(x, 'context', [(i, (i + step) % size) for i in range(size)])  8.88 us
    another operation x2, other arithmetic, gathered(): return (jnp.stack(turned), (me - jnp.arange(size, dtype=jnp.int32)) % size)  4.15 us
    dot_general x6, matrix products, unit_lower_inverse(): jnp.einsum('hij,hjk->hik', inverse, half, precision=HIGH)  4.08 us
    dot_general x6, matrix products, unit_lower_inverse(): half = jnp.einsum('hij,hjk->hik', cross, inverse, precision=HIGH)  4 us
    dot_general x3, matrix products, shards(): jnp.einsum('hik,hvk->hiv', jnp.where(select[owner][None, :, None], weight...  2.89 us
    unnamed x59, local copies, waits for them, and re-layouts  2.53 us
    dot_general x1, matrix products, shards(): jnp.einsum('hjk,hj,hjl->hkl', wy_keys, end_weight, key_heads_first, preci...  2.48 us
  transfers between devices with their start and end apart: 6, of which 0 were waited for; matrix products, arithmetic and copies ran while one was open for 60% of the time, Pallas kernels for 17%

profile of v2, /device:TPU:28, one launch (start us, length us, event | category | flops | bytes accessed | tf_op | source)
XLA Modules:
  0.0 93.9 jit_solution(9088951955089201917)
XLA Ops:
  1.5 3.0 %collective-permute-start = (bf16[2,8,32,128]{3,2,1,0:T(8,128)(2,1)}, bf16[2,8,32,128]{3,2,1,0:T(8,128)(2,1)}, u32[]{:S(2)}, u32[]{:S(2)}) collective-permute-start(bf16[2,8,32,128]{3,2,1,0:T(8,128)(2,1)} %param.25), channel_id=1, source_target_pairs={{0,4},{4,8},{8,12},{12,0},{1,5},{5,9},{9,13},{13,1},{2,6},{6,10},{... | collective-permute-start | bytes 393224 | tf_op jit(solution)/shard_map/ppermute | solution.py:90
  4.6 0.8 reduce-window.9
  6.2 0.9 constant_dynamic-slice_fusion.1
  7.2 0.9 constant_dynamic-slice_fusion
  8.5 0.8 select_reduce_fusion.1
  9.5 0.8 reshape.1611
  10.8 1.5 %collective-permute-start.4 = (bf16[2,256,256]{1,0,2:T(2,128)(2,1)}, bf16[2,256,256]{1,0,2:T(2,128)(2,1)}, u32[]{:S(2)}, u32[]{:S(2)}) collective-permute-start(bf16[2,256,256]{1,0,2:T(2,128)(2,1)} %reshape.1611), channel_id=1, source_target_pairs={{0,8},{4,12},{8,0},{12,4},{1,9},{5,13},{9,1},{13,5},{2,10},{6,14},... | collective-permute-start | bytes 786440 | tf_op jit(solution)/shard_map/ppermute | solution.py:90
  15.3 0.8 fusion.81
  19.0 1.2 %fusion.9 = f32[8,128,128]{2,1,0:T(8,128)S(1)} fusion(f32[8,128,128]{2,1,0:T(8,128)S(1)} %bitcast.129, f32[8,128]{1,0:T(8,128)S(1)} %divide_bitcast_fusion, f32[8,128]{1,0:T(8,128)S(1)} %convolution_bitcast_fusion, pred[128,128]{1,0:T(8,128)(4,1)S(1)} %get-tuple-element.37, pred[128,128]{1,0:T(8,128)(4,1)S(1)} %get-tuple-element.36), kind=kOutput, calls=%fused_computation.24 | convolution fusion | flops 202113024 | bytes 1089536 | tf_op jit(solution)/shard_map/hid,hjd->hij/dot_general | solution.py:252
  20.3 0.7 fusion.33
  21.0 0.7 convolution_subtract_fusion.5
  22.4 0.7 convolution_subtract_fusion.4
  23.9 0.7 convolution_subtract_fusion.3
  26.8 0.7 convolution_subtract_fusion.1
  28.3 0.7 convolution_subtract_fusion
  29.0 1.8 %fusion.123 = (pred[128]{0:T(512)(128)(4,1)S(1)}, pred[128]{0:T(512)(128)(4,1)}, pred[128]{0:T(512)(128)(4,1)S(1)}) fusion(pred[]{:T(512)S(6)} %lt.59, s32[]{:T(128)} %bitcast.11, s32[128]{0:T(128)S(1)} %convert_reduce_fusion.1, s32[]{:T(128)} %bitcast.25), kind=kLoop, calls=%fused_computation.277 | loop fusion | flops 640 | bytes 905 | tf_op jit(solution)/shard_map/not | solution.py:294
  30.8 0.7 slice_reduce_fusion.1
  32.1 1.4 %convolution_multiply_fusion.1 = f32[8,128,128]{2,1,0:T(8,128)S(1)} fusion(f32[8,128,128]{2,1,0:T(8,128)S(1)} %bitcast.131, f32[8,128,128]{2,1,0:T(8,128)S(1)} %bitcast.130, f32[8,128]{1,0:T(8,128)S(1)} %convolution_bitcast_fusion, pred[128,128]{1,0:T(8,128)(4,1)S(1)} %get-tuple-element.36), kind=kOutput, calls=%fused_computation.25 | convolution fusion | flops 201850880 | bytes 1593344 | tf_op jit(solution)/shard_map/hid,hjd->hij/dot_general | solution.py:253
  34.0 1.0 %fusion.14 = f32[8,128,256]{2,1,0:T(8,128)S(1)} fusion(f32[8,128,128]{2,1,0:T(8,128)S(1)} %convolution_subtract_fusion, f32[8,128,128]{2,1,0:T(8,128)S(1)} %get-tuple-element.23, f32[8,128,128]{2,1,0:T(8,128)S(1)} %get-tuple-element.69), kind=kOutput, calls=%fused_computation.31 | convolution fusion | flops 402915328 | bytes 2621440 | tf_op jit(solution)/shard_map/hij,hjk->hik/dot_general | solution.py:258
  35.1 1.8 %fusion.37 = f32[8,128,128]{2,1,0:T(8,128)} fusion(f32[8,128,128]{2,1,0:T(8,128)S(1)} %get-tuple-element.24, f32[8,128,256]{2,1,0:T(8,128)S(1)} %fusion.14), kind=kOutput, calls=%fused_computation.65 | convolution fusion | flops 201326592 | bytes 1572864 | tf_op jit(solution)/shard_map/hjv,hj,hjl->hvl/dot_general | solution.py:279
  36.9 0.7 fusion.12
  38.5 0.9 %add_divide_fusion = f32[128,1024]{0,1:T(8,128)} fusion(bf16[128,1024]{0,1:T(8,128)(2,1)S(1)} %copy.119), kind=kLoop, calls=%fused_computation.44 | loop fusion | flops 524288 | bytes 786432 | tf_op jit(solution)/shard_map/div | solution.py:345
  40.6 0.8 copy.111
  41.4 1.4 %copy.110 = f32[128,32]{1,0:T(8,128)} copy(f32[128,32]{0,1:T(8,128)} %get-tuple-element.34) | data formatting | bytes 32768 | tf_op jit(solution)/shard_map/mul | solution.py:129
  42.9 2.5 %broadcast_select_fusion = (bf16[8,128,128]{2,1,0:T(8,128)(2,1)}, bf16[8,128,128]{2,1,0:T(8,128)(2,1)}) fusion(pred[]{:T(512)S(6)} %ge.31, f32[8,128,128]{2,1,0:T(8,128)S(1)} %get-tuple-element.24, f32[8,128,256]{2,1,0:T(8,128)S(1)} %fusion.14, f32[128,128]{1,0:T(8,128)S(1)} %fusion.80, f32[8]{0:T(128)} %slice_reduce_fusion.1), kind=kOutput, calls=%fused_computation.104 | convolution fusion | flops 201850880 | bytes 1638433 | tf_op jit(solution)/shard_map/hjk,hj,hjl->hkl/dot_general | solution.py:276
  45.3 1.1 %compare_and_fusion = pred[128,4,128]{2,1,0:T(4,128)(4,1)S(1)} fusion(s32[4,128]{1,0:T(4,128)S(1)} %get-tuple-element.39, s32[4,128]{1,0:T(4,128)S(1)} %add_bitcast_fusion, s32[128]{0:T(128)} %copy-done.17, s32[128]{0:T(128)S(1)} %broadcast_add_fusion), kind=kLoop, calls=%fused_computation.100 | loop fusion | flops 196608 | bytes 70656 | tf_op jit(solution)/shard_map/and | solution.py:336
  46.4 0.8 select_reduce_fusion
  47.8 1.0 %compare_and_fusion.1 = pred[128,4,128]{2,1,0:T(4,128)(4,1)S(1)} fusion(s32[4,128]{1,0:T(4,128)S(1)} %get-tuple-element.33, s32[4,128]{1,0:T(4,128)S(1)} %get-tuple-element.32, s32[128]{0:T(128)} %copy-done.18, s32[128]{0:T(128)} %copy-done.19), kind=kLoop, calls=%fused_computation.101 | loop fusion | flops 196608 | bytes 70656 | tf_op jit(solution)/shard_map/and | solution.py:335
  48.8 0.8 pad_add_fusion
  49.6 0.8 subtract_convert_fusion
  50.5 1.3 %slice.81 = s32[1]{0:T(128)} slice(s32[128]{0:T(128)} %copy-done.19), slice={[127:128]} | slice | bytes 8 | tf_op jit(solution)/shard_map/slice | solution.py:281
  51.8 0.8 stack_reshape.3
  52.6 0.8 slice.98
  53.4 1.1 %copy.107 = f32[128,1024]{0,1:T(8,128)S(1)} copy(bf16[128,1024]{1,0:T(8,128)(2,1)} %param.21) | data formatting | bytes 786432 | tf_op jit(solution)/shard_map/convert_element_type | solution.py:308
  55.7 1.0 %copy.120 = f32[128,4,256]{2,0,1:T(8,128)} copy(f32[128,4,256]{0,2,1:T(8,128)S(1)} %bitcast.138) | data formatting | bytes 1048576 | tf_op jit(solution)/shard_map/div | solution.py:345
  56.8 3.0 %collective-permute-start.3 = (bf16[2,256,256]{1,0,2:T(2,128)(2,1)}, bf16[2,256,256]{1,0,2:T(2,128)(2,1)}, u32[]{:S(2)}, u32[]{:S(2)}) collective-permute-start(bf16[2,256,256]{1,0,2:T(2,128)(2,1)} %reshape.1611), channel_id=1, source_target_pairs={{0,4},{4,8},{8,12},{12,0},{1,5},{5,9},{9,13},{13,1},{2,6},{6,10},{... | collective-permute-start | bytes 786440 | tf_op jit(solution)/shard_map/ppermute | solution.py:90
  59.7 1.1 %pad_maximum_fusion.1 = bf16[4,2,8,32,128]{4,3,2,1,0:T(8,128)(2,1)S(1)} fusion(bf16[1,2,8,32,128]{4,3,2,1,0:T(8,128)(2,1)} %bitcast.18, bf16[1,2,8,32,128]{4,3,2,1,0:T(8,128)(2,1)} %bitcast.17, bf16[1,2,8,32,128]{4,3,2,1,0:T(8,128)(2,1)} %bitcast.16, bf16[1,2,8,32,128]{4,3,2,1,0:T(8,128)(2,1)S(1)} %bitcast.152), kind=kLoop, calls=%fused_computation.40 | loop fusion | flops 786432 | bytes 1048576 | tf_op jit(solution)/shard_map/stack | solution.py:93
  62.2 1.2 %fusion.52 = f32[8,128,128]{1,2,0:T(8,128)} fusion(bf16[8,128,128]{2,1,0:T(8,128)(2,1)S(1)} %bitcast.135, bf16[8,128,128]{2,1,0:T(8,128)(2,1)S(1)} %fusion.12, pred[128]{0:T(512)(128)(4,1)S(1)} %copy-done.21), kind=kOutput, calls=%fused_computation.83 | convolution fusion | flops 33685504 | bytes 1048704 | tf_op jit(solution)/shard_map/hik,hvk->hiv/dot_general | solution.py:300
  63.4 1.0 %fusion.4.refs_1_ = f32[8,128,128]{2,1,0:T(8,128)} fusion(f32[8,128,128]{2,1,0:T(8,128)S(1)} %copy-done.1, bf16[8,128,128]{2,1,0:T(8,128)(2,1)S(1)} %copy-done.3, bf16[8,128,128]{2,1,0:T(8,128)(2,1)S(1)} %bitcast.134, bf16[8,128,128]{2,1,0:T(8,128)(2,1)S(1)} %bitcast.136, pred[]{:T(512)} %bitcast.27, pred[]{:T(512)} %bitcast.26, pred[]{:T(512)S(6)} %ge.31), kind=kOutput, calls=%fused_computation.15 | convolution fusion | flops 34078720 | bytes 1835011 | tf_op jit(solution)/shard_map/hvj,hjk->hvk/dot_general | solution.py:286
  64.4 15.9 %shard_map.185 = bf16[8,128,128]{2,1,0:T(8,128)(2,1)} custom-call(bf16[8,128,128]{2,1,0:T(8,128)(2,1)} %get-tuple-element.49.refs_0_, f32[8,128,128]{2,1,0:T(8,128)} %fusion.4.refs_1_), custom_call_target="tpu_custom_call" | custom-call | tf_op jit(solution)/shard_map/pallas_call | solution.py:73
  80.3 1.3 %fusion.48 = f32[8,128,128]{1,2,0:T(8,128)S(1)} fusion(bf16[8,128,128]{2,1,0:T(8,128)(2,1)} %shard_map.185, bf16[8,128,128]{2,1,0:T(8,128)(2,1)S(1)} %fusion.12, pred[128]{0:T(512)(128)(4,1)S(1)} %copy-done.20), kind=kOutput, calls=%fused_computation.79 | convolution fusion | flops 33685504 | bytes 1048704 | tf_op jit(solution)/shard_map/hik,hvk->hiv/dot_general | solution.py:300
  81.6 2.1 %multiply_reduce_fusion = (f32[128,8]{0,1:T(8,128)S(1)}, f32[128,8,128]{0,2,1:T(8,128)S(1)}) fusion(f32[8,128,128]{1,2,0:T(8,128)S(1)} %fusion.48, f32[8,128,128]{1,2,0:T(8,128)S(1)} %fusion.50, f32[8,128,128]{1,2,0:T(8,128)} %fusion.52, f32[8,128,128]{2,1,0:T(8,128)S(1)} %convolution_multiply_fusion.1, f32[8,128,256]{2,1,0:T(8,128)S(1)} %fusion.14), kind=kOutput, calls=%fused_computation.46 | convolution fusion | flops 201980928 | bytes 3149824 | tf_op jit(solution)/shard_map/hij,hjv->hiv/dot_general | solution.py:267
  84.0 0.9 copy.122
  84.8 3.1 %pad_maximum_fusion = bf16[4,2,256,256]{2,1,3,0:T(2,128)(2,1)S(1)} fusion(bf16[1,2,256,256]{2,1,3,0:T(2,128)(2,1)} %bitcast.42, bf16[1,2,256,256]{2,1,3,0:T(2,128)(2,1)} %bitcast.41, bf16[1,2,256,256]{2,1,3,0:T(2,128)(2,1)} %bitcast.40, bf16[1,2,256,256]{2,1,3,0:T(2,128)(2,1)} %stack_reshape.3), kind=kLoop, calls=%fused_computation.35 | loop fusion | flops 1572864 | bytes 2097152 | tf_op jit(solution)/shard_map/stack | solution.py:93
  87.9 1.5 %fusion.124 = (bf16[4,1,256,256]{2,1,3,0:T(2,128)(2,1)S(1)}, bf16[4,1,256,256]{2,1,3,0:T(2,128)(2,1)S(1)}) fusion(bf16[4,2,256,256]{2,1,3,0:T(2,128)(2,1)S(1)} %pad_maximum_fusion), kind=kLoop, calls=%fused_computation.278 | loop fusion | bytes 2097152 | tf_op jit(solution)/shard_map/slice | solution.py:339
  91.4 0.7 fusion.1
  92.1 0.8 fusion.11
  93.1 0.9 copy.123
  (148 shorter events, 19.2 us)
Async XLA Ops:
  0.6 16.1 %copy-start = (f32[128,8]{0,1:T(8,128)S(1)}, f32[128,8]{0,1:T(8,128)}, u32[]{:S(2)}) copy-start(f32[128,8]{0,1:T(8,128)} %param.23) | copy-start | bytes 12292
  0.6 17.2 %copy-start.11 = (bf16[128,512]{1,0:T(8,128)(2,1)S(1)}, bf16[128,512]{1,0:T(8,128)(2,1)}, u32[]{:S(2)}) copy-start(bf16[128,512]{1,0:T(8,128)(2,1)} %param.19) | copy-start | bytes 393220
  0.7 56.1 %collective-permute-start.2 = (bf16[2,8,32,128]{3,2,1,0:T(8,128)(2,1)}, bf16[2,8,32,128]{3,2,1,0:T(8,128)(2,1)}, u32[]{:S(2)}, u32[]{:S(2)}) collective-permute-start(bf16[2,8,32,128]{3,2,1,0:T(8,128)(2,1)} %param.25), channel_id=1, source_target_pairs={{0,12},{4,0},{8,4},{12,8},{1,13},{5,1},{9,5},{13,9},{2,14},{6,2},{... | collective-permute-start | bytes 393224 | tf_op jit(solution)/shard_map/ppermute | solution.py:90
  1.2 58.6 %collective-permute-start.1 = (bf16[2,8,32,128]{3,2,1,0:T(8,128)(2,1)}, bf16[2,8,32,128]{3,2,1,0:T(8,128)(2,1)}, u32[]{:S(2)}, u32[]{:S(2)}) collective-permute-start(bf16[2,8,32,128]{3,2,1,0:T(8,128)(2,1)} %param.25), channel_id=1, source_target_pairs={{0,8},{4,12},{8,0},{12,4},{1,9},{5,13},{9,1},{13,5},{2,10},{6,14},... | collective-permute-start | bytes 393224 | tf_op jit(solution)/shard_map/ppermute | solution.py:90
  1.5 58.2 %collective-permute-start = (bf16[2,8,32,128]{3,2,1,0:T(8,128)(2,1)}, bf16[2,8,32,128]{3,2,1,0:T(8,128)(2,1)}, u32[]{:S(2)}, u32[]{:S(2)}) collective-permute-start(bf16[2,8,32,128]{3,2,1,0:T(8,128)(2,1)} %param.25), channel_id=1, source_target_pairs={{0,4},{4,8},{8,12},{12,0},{1,5},{5,9},{9,13},{13,1},{2,6},{6,10},{... | collective-permute-start | bytes 393224 | tf_op jit(solution)/shard_map/ppermute | solution.py:90
  4.6 13.9 %copy-start.17 = (s32[128]{0:T(128)}, s32[128]{0:T(128)S(1)}, u32[]{:S(2)}) copy-start(s32[128]{0:T(128)S(1)} %iota_add_fusion.2) | copy-start | bytes 1540
  8.1 10.4 %copy-start.7 = (bf16[128,1024]{1,0:T(8,128)(2,1)S(1)}, bf16[128,1024]{1,0:T(8,128)(2,1)}, u32[]{:S(2)}) copy-start(bf16[128,1024]{1,0:T(8,128)(2,1)} %param.20) | copy-start | bytes 786436
  9.2 9.6 %copy-start.18 = (s32[128]{0:T(128)}, s32[128]{0:T(128)S(1)}, u32[]{:S(2)}) copy-start(s32[128]{0:T(128)S(1)} %get-tuple-element.12) | copy-start | bytes 1540
  9.2 28.4 %copy-start.19 = (s32[128]{0:T(128)}, s32[128]{0:T(128)S(1)}, u32[]{:S(2)}) copy-start(s32[128]{0:T(128)S(1)} %get-tuple-element.14) | copy-start | bytes 1540
  9.5 9.3 %copy-start.16 = (f32[128,8]{0,1:T(8,128)S(1)}, f32[128,8]{0,1:T(8,128)}, u32[]{:S(2)}) copy-start(f32[128,8]{0,1:T(8,128)} %param.22) | copy-start | bytes 12292
  10.3 74.6 %collective-permute-start.5 = (bf16[2,256,256]{1,0,2:T(2,128)(2,1)}, bf16[2,256,256]{1,0,2:T(2,128)(2,1)}, u32[]{:S(2)}, u32[]{:S(2)}) collective-permute-start(bf16[2,256,256]{1,0,2:T(2,128)(2,1)} %reshape.1611), channel_id=1, source_target_pairs={{0,12},{4,0},{8,4},{12,8},{1,13},{5,1},{9,5},{13,9},{2,14},{6,2},{... | collective-permute-start | bytes 786440 | tf_op jit(solution)/shard_map/ppermute | solution.py:90
  10.8 74.0 %collective-permute-start.4 = (bf16[2,256,256]{1,0,2:T(2,128)(2,1)}, bf16[2,256,256]{1,0,2:T(2,128)(2,1)}, u32[]{:S(2)}, u32[]{:S(2)}) collective-permute-start(bf16[2,256,256]{1,0,2:T(2,128)(2,1)} %reshape.1611), channel_id=1, source_target_pairs={{0,8},{4,12},{8,0},{12,4},{1,9},{5,13},{9,1},{13,5},{2,10},{6,14},... | collective-permute-start | bytes 786440 | tf_op jit(solution)/shard_map/ppermute | solution.py:90
  26.8 4.7 %copy-start.12 = (bf16[128,512]{1,0:T(8,128)(2,1)S(1)}, bf16[128,512]{1,0:T(8,128)(2,1)}, u32[]{:S(2)}) copy-start(bf16[128,512]{1,0:T(8,128)(2,1)} %param.18) | copy-start | bytes 393220
  35.1 3.2 %copy-start.8 = (bf16[128,1024]{1,0:T(8,128)(2,1)S(1)}, bf16[128,1024]{1,0:T(8,128)(2,1)}, u32[]{:S(2)}) copy-start(bf16[128,1024]{1,0:T(8,128)(2,1)} %param.27) | copy-start | bytes 786436
  35.1 4.5 %copy-start.25 = (s32[4]{0:T(128)S(1)}, s32[4]{0:T(128)}, u32[]{:S(2)}) copy-start(s32[4]{0:T(128)} %get-tuple-element.56) | copy-start | bytes 52
  35.1 5.1 %copy-start.9 = (bf16[128,1024]{1,0:T(8,128)(2,1)S(1)}, bf16[128,1024]{1,0:T(8,128)(2,1)}, u32[]{:S(2)}) copy-start(bf16[128,1024]{1,0:T(8,128)(2,1)} %param.26) | copy-start | bytes 786436
  42.9 6.8 %copy-start.6 = (f32[128,32]{1,0:T(8,128)S(1)}, f32[128,32]{1,0:T(8,128)}, u32[]{:S(2)}) copy-start(f32[128,32]{1,0:T(8,128)} %copy.110) | copy-start | bytes 49156
  45.3 10.3 %copy-start.2 = (f32[128,1024]{0,1:T(8,128)S(1)}, f32[128,1024]{0,1:T(8,128)}, u32[]{:S(2)}) copy-start(f32[128,1024]{0,1:T(8,128)} %add_divide_fusion) | copy-start | bytes 1572868
  49.6 7.1 %copy-start.24 = (s32[4]{0:T(128)S(1)}, s32[4]{0:T(128)}, u32[]{:S(2)}) copy-start(s32[4]{0:T(128)} %fusion.104) | copy-start | bytes 52
  50.5 6.2 %copy-start.5 = (pred[128,4,256]{2,1,0:T(4,128)(4,1)S(1)}, pred[128,4,256]{2,1,0:T(4,128)(4,1)}, u32[]{:S(2)}) copy-start(pred[128,4,256]{2,1,0:T(4,128)(4,1)} %pad_add_fusion) | copy-start | bytes 393220
  50.5 9.3 %copy-start.15 = (bf16[2,8,32,128]{3,2,1,0:T(8,128)(2,1)S(1)}, bf16[2,8,32,128]{3,2,1,0:T(8,128)(2,1)}, u32[]{:S(2)}) copy-start(bf16[2,8,32,128]{3,2,1,0:T(8,128)(2,1)} %param.25) | copy-start | bytes 393220
  56.8 28.1 %collective-permute-start.3 = (bf16[2,256,256]{1,0,2:T(2,128)(2,1)}, bf16[2,256,256]{1,0,2:T(2,128)(2,1)}, u32[]{:S(2)}, u32[]{:S(2)}) collective-permute-start(bf16[2,256,256]{1,0,2:T(2,128)(2,1)} %reshape.1611), channel_id=1, source_target_pairs={{0,4},{4,8},{8,12},{12,0},{1,5},{5,9},{9,13},{13,1},{2,6},{6,10},{... | collective-permute-start | bytes 786440 | tf_op jit(solution)/shard_map/ppermute | solution.py:90
  60.8 0.9 copy-start.22
  61.5 0.6 copy-start.21
  61.6 1.7 %copy-start.1 = (f32[8,128,128]{2,1,0:T(8,128)S(1)}, f32[8,128,128]{2,1,0:T(8,128)}, u32[]{:S(2)}) copy-start(f32[8,128,128]{2,1,0:T(8,128)} %fusion.37) | copy-start | bytes 1572868
  61.7 1.7 %copy-start.3 = (bf16[8,128,128]{2,1,0:T(8,128)(2,1)S(1)}, bf16[8,128,128]{2,1,0:T(8,128)(2,1)}, u32[]{:S(2)}) copy-start(bf16[8,128,128]{2,1,0:T(8,128)(2,1)} %get-tuple-element.50) | copy-start | bytes 786436
  62.2 18.1 %copy-start.20 = (pred[128]{0:T(512)(128)(4,1)S(1)}, pred[128]{0:T(512)(128)(4,1)}, u32[]{:S(2)}) copy-start(pred[128]{0:T(512)(128)(4,1)} %get-tuple-element.16) | copy-start | bytes 388
  80.3 3.4 %copy-start.23 = (f32[128]{0:T(128)S(1)}, f32[128]{0:T(128)}, u32[]{:S(2)}) copy-start(f32[128]{0:T(128)} %param.24) | copy-start | bytes 1540
  89.4 1.3 %copy-start.10 = (bf16[128,4,192]{2,0,1:T(8,128)(2,1)S(1)}, bf16[128,4,192]{2,0,1:T(8,128)(2,1)}, u32[]{:S(2)}) copy-start(bf16[128,4,192]{2,0,1:T(8,128)(2,1)} %slice.98) | copy-start | bytes 589828
  89.4 1.3 %copy-start.13 = (bf16[128,4,32]{2,0,1:T(8,128)(2,1)S(1)}, bf16[128,4,32]{2,0,1:T(8,128)(2,1)}, u32[]{:S(2)}) copy-start(bf16[128,4,32]{2,0,1:T(8,128)(2,1)} %get-tuple-element.19) | copy-start | bytes 98308
  89.4 1.3 %copy-start.14 = (bf16[128,4,32]{2,0,1:T(8,128)(2,1)S(1)}, bf16[128,4,32]{2,0,1:T(8,128)(2,1)}, u32[]{:S(2)}) copy-start(bf16[128,4,32]{2,0,1:T(8,128)(2,1)} %get-tuple-element.20) | copy-start | bytes 98308
  90.7 1.4 %copy-start.4 = (f32[128,4,256]{2,0,1:T(8,128)S(1)}, f32[128,4,256]{2,0,1:T(8,128)}, u32[]{:S(2)}) copy-start(f32[128,4,256]{2,0,1:T(8,128)} %copy.120) | copy-start | bytes 1572868

commit v3 on v2

--- a/solution.py
+++ b/solution.py
@@ -93,21 +93,130 @@
     return jnp.stack(turned), (me - jnp.arange(size, dtype=jnp.int32)) % size
 
 
-def unit_lower_inverse(lower):
-    size = lower.shape[-1]
-    index = jnp.arange(size)
-    inverse = jnp.eye(size, dtype=jnp.float32)[None] - jnp.where(
-        (index[:, None] // 2 == index[None, :] // 2)[None], lower, 0.0
-    )
+def halves(x):
+    high = x.astype(jnp.bfloat16)
+    return high, (x - high.astype(jnp.float32)).astype(jnp.bfloat16)
+
+
+def dot1(a, b, contract=((1,), (0,))):
+    return lax.dot_general(a, b, (contract, ((), ())), preferred_element_type=jnp.float32)
+
+
+def dot2(a, exact):
+    high, low = halves(a)
+    return dot1(high, exact) + dot1(low, exact)
+
+
+def dot3(a, b):
+    a_high, a_low = halves(a)
+    b_high, b_low = halves(b)
+    return dot1(a_high, b_high) + (dot1(a_high, b_low) + dot1(a_low, b_high))
+
+
+def local_kernel(
+    query_ref, key_ref, value_ref, logit_ref, logit_row_ref, decay_ref, decay_row_ref,
+    seg_ref, seg_row_ref, local_ref, reach_ref, map_ref, add_ref,
+):
+    tokens = query_ref.shape[0]
+    heads = local_ref.shape[0]
+    share = VH // KH
+    seg, seg_row = seg_ref[...], seg_row_ref[...]
+    row = lax.broadcasted_iota(jnp.int32, (tokens, tokens), 0)
+    col = lax.broadcasted_iota(jnp.int32, (tokens, tokens), 1)
+    same = seg == seg_row
+    causal = same & (row >= col)
+    strict = same & (row > col)
+    eye = row == col
+    causal_f = causal.astype(jnp.float32)
+    run = lax.dot_general(
+        causal_f, decay_ref[...], (((1,), (0,)), ((), ())),
+        precision=HIGH, preferred_element_type=jnp.float32,
+    )
+    run_row = lax.dot_general(
+        decay_row_ref[...], causal_f, (((1,), (1,)), ((), ())),
+        precision=HIGH, preferred_element_type=jnp.float32,
+    )
+    beta, beta_row = jax.nn.sigmoid(logit_ref[...]), jax.nn.sigmoid(logit_row_ref[...])
+    start, start_row = jnp.exp(run), jnp.exp(run_row)
+    tail = seg_row == seg_row[:, tokens - 1 : tokens]
+    end_row = jnp.where(
+        tail, jnp.exp(jnp.where(tail, run_row[:, tokens - 1 : tokens] - run_row, 0.0)), 0.0
+    )
+    keys, grams, mixes, scaled, inv_rows = [], [], [], [], []
+    for g in range(heads // share):
+        k = key_ref[:, g * DK : (g + 1) * DK]
+        q = query_ref[:, g * DK : (g + 1) * DK]
+        gram = dot1(k, k, ((1,), (1,)))
+        cross = dot1(q, k, ((1,), (1,)))
+        squares = jnp.where(eye, gram, 0.0)
+        inv = lax.rsqrt(jnp.sum(squares, axis=1, keepdims=True) + 1e-06)
+        inv_row = lax.rsqrt(jnp.sum(squares, axis=0, keepdims=True) + 1e-06)
+        q_f = q.astype(jnp.float32)
+        inv_q = lax.rsqrt(jnp.sum(q_f * q_f, axis=1, keepdims=True) + 1e-06) * DK ** (-0.5)
+        keys.append(k)
+        inv_rows.append(inv_row)
+        grams.append(gram * inv * inv_row)
+        mixes.append(cross * inv_q * inv_row)
+        scaled.append(q_f * inv_q)
+    lowers, inverses, mixing = [], [], []
+    for h in range(heads):
+        gaps = run[:, h : h + 1] - run_row[h : h + 1, :]
+        decay_mat = jnp.where(causal, jnp.exp(jnp.where(causal, gaps, 0.0)), 0.0)
+        mixing.append(decay_mat * mixes[h // share])
+        lower = jnp.where(strict, beta[:, h : h + 1] * grams[h // share] * decay_mat, 0.0)
+        lowers.append(lower)
+        inverses.append(
+            jnp.where(eye, 1.0, 0.0) - jnp.where(row // 2 == col // 2, lower, 0.0)
+        )
     width = 2
-    while width < size:
-        block = index // width
-        pair = (block[:, None] // 2 == block[None, :] // 2) & (block[:, None] > block[None, :])
-        cross = jnp.where(pair[None], lower, 0.0)
-        half = jnp.einsum("hij,hjk->hik", cross, inverse, precision=HIGH)
-        inverse = inverse - jnp.einsum("hij,hjk->hik", inverse, half, precision=HIGH)
+    while width < tokens:
+        pair = (row // (2 * width) == col // (2 * width)) & (row // width > col // width)
+        half = [dot3(jnp.where(pair, lowers[h], 0.0), inverses[h]) for h in range(heads)]
+        inverses = [inverses[h] - dot3(inverses[h], half[h]) for h in range(heads)]
         width *= 2
-    return inverse
+    for h in range(heads):
+        g = h // share
+        weighted = inverses[h] * beta_row[h : h + 1, :]
+        update = dot2(weighted, value_ref[:, h * DV : (h + 1) * DV])
+        wy = dot2(weighted * (start_row[h : h + 1, :] * inv_rows[g]), keys[g])
+        solved = jnp.concatenate([update, wy], axis=1)
+        mixed = dot3(mixing[h], solved)
+        local_ref[h] = mixed[:, :DV]
+        reach_ref[h] = (start[:, h : h + 1] * scaled[g] - mixed[:, DV:]).astype(jnp.bfloat16)
+        turned = solved.T * (end_row[h : h + 1, :] * inv_rows[g])
+        carry = dot2(turned, keys[g])
+        add_ref[h] = carry[:DV]
+        map_ref[h] = (
+            jnp.where(eye, start[tokens - 1 : tokens, h : h + 1], 0.0) - carry[DV:]
+        ).astype(jnp.bfloat16)
+
+
+def finish_kernel(local_ref, reach_ref, states_ref, into_ref, select_ref, gate_ref, gain_ref, out_ref):
+    owners = states_ref.shape[0]
+    select = select_ref[...] > 0.5
+    for h in range(local_ref.shape[0]):
+        core = local_ref[h]
+        reach = reach_ref[h]
+        for owner in range(owners + 1):
+            state = states_ref[owner, h] if owner < owners else into_ref[h]
+            part = dot1(reach, state, ((1,), (1,)))
+            core = core + jnp.where(select[:, owner : owner + 1], part, 0.0)
+        normed = core * lax.rsqrt(jnp.mean(core * core, axis=1, keepdims=True) + 1e-06)
+        gate = gate_ref[:, h * DV : (h + 1) * DV].astype(jnp.float32)
+        out_ref[:, h * DV : (h + 1) * DV] = (
+            normed * gain_ref[...] * (gate * jax.nn.sigmoid(gate))
+        ).astype(jnp.bfloat16)
+
+
+def whole_call(kernel, shapes, *arrays):
+    space = pl.BlockSpec(memory_space=pltpu.VMEM)
+    return pl.pallas_call(
+        kernel,
+        out_shape=shapes,
+        in_specs=[space] * len(arrays),
+        out_specs=jax.tree.map(lambda _: space, shapes),
+        compiler_params=pltpu.CompilerParams(vmem_limit_bytes=48 * 2**20),
+    )(*arrays)
 
 
 def yarn_tables(positions, rotary):
@@ -139,10 +248,6 @@
         [first * cosines - second * sines, second * cosines + first * sines, values[..., rotary:]],
         axis=-1,
     )
-
-
-def unit_rows(values):
-    return values * lax.rsqrt(jnp.sum(values * values, axis=-1, keepdims=True) + 1e-06)
 
 
 def row_layout(rows, req_len, req_prefix, req_offset):
@@ -196,7 +301,6 @@
     block_table,
 ):
     tokens_here = dn_query.shape[0]
-    key_heads = dn_query.shape[1] // DK
     value_heads = dn_value.shape[1] // DV
     query_heads = at_query.shape[1] // HD
     device = lax.axis_index("context")
@@ -229,60 +333,30 @@
         device,
     )
     cached_rows = cached_key.shape[0] * cached_key.shape[1]
-    query = jnp.repeat(
-        unit_rows(dn_query.reshape(tokens_here, key_heads, DK).astype(jnp.float32)) * DK ** (-0.5),
-        VH // KH,
-        axis=1,
-    )
-    key = jnp.repeat(
-        unit_rows(dn_key.reshape(tokens_here, key_heads, DK).astype(jnp.float32)), VH // KH, axis=1
-    )
-    query_heads_first = jnp.transpose(query, (1, 0, 2))
-    key_heads_first = jnp.transpose(key, (1, 0, 2))
-    value_heads_first = jnp.transpose(
-        dn_value.reshape(tokens_here, value_heads, DV).astype(jnp.float32), (1, 0, 2)
-    )
-    beta = jax.nn.sigmoid(dn_beta_logit).T
-    same = segment[:, None] == segment[None, :]
-    causal = same & (rows[:, None] >= rows[None, :])
-    strict = same & (rows[:, None] > rows[None, :])
-    running = jnp.dot(causal.astype(jnp.float32), dn_decay, precision=HIGH).T
-    gaps = running[:, :, None] - running[:, None, :]
-    decay_mat = jnp.where(causal[None], jnp.exp(jnp.where(causal[None], gaps, 0.0)), 0.0)
-    key_gram = jnp.einsum("hid,hjd->hij", key_heads_first, key_heads_first, precision=HIGH)
-    query_key = jnp.einsum("hid,hjd->hij", query_heads_first, key_heads_first, precision=HIGH)
-    lower_mat = jnp.where(strict[None], beta[:, :, None] * key_gram * decay_mat, 0.0)
-    start_decay = jnp.exp(running)
-    solve_values = beta[:, :, None] * value_heads_first
-    solve_keys = (beta * start_decay)[:, :, None] * key_heads_first
-    solved = jnp.einsum(
-        "hij,hjk->hik",
-        unit_lower_inverse(lower_mat),
-        jnp.concatenate([solve_values, solve_keys], axis=2),
-        precision=HIGH,
-    )
-    update = solved[:, :, :DV]
-    wy_keys = solved[:, :, DV:]
-    mixing = decay_mat * query_key
-    local_out = jnp.einsum("hij,hjv->hiv", mixing, update, precision=HIGH)
-    reach = start_decay[:, :, None] * query_heads_first - jnp.einsum(
-        "hij,hjk->hik", mixing, wy_keys, precision=HIGH
-    )
-    tail = segment == segment[tokens_here - 1]
-    end_gaps = running[:, tokens_here - 1 : tokens_here] - running
-    end_weight = jnp.where(tail[None, :], jnp.exp(jnp.where(tail[None, :], end_gaps, 0.0)), 0.0)
-    end_decay = start_decay[:, tokens_here - 1]
-    identity_mat = jnp.eye(DK, dtype=jnp.float32)
-    carry_map = end_decay[:, None, None] * identity_mat[None] - jnp.einsum(
-        "hjk,hj,hjl->hkl", wy_keys, end_weight, key_heads_first, precision=HIGH
-    )
-    carry_add = jnp.einsum("hjv,hj,hjl->hvl", update, end_weight, key_heads_first, precision=HIGH)
+    square = (value_heads, DK, DK)
+    local_out, reach, map_half, carry_add = whole_call(
+        local_kernel,
+        [
+            jax.ShapeDtypeStruct((value_heads, tokens_here, DV), jnp.float32),
+            jax.ShapeDtypeStruct((value_heads, tokens_here, DK), jnp.bfloat16),
+            jax.ShapeDtypeStruct(square, jnp.bfloat16),
+            jax.ShapeDtypeStruct(square, jnp.float32),
+        ],
+        dn_query,
+        dn_key,
+        dn_value,
+        dn_beta_logit,
+        dn_beta_logit.T,
+        dn_decay,
+        dn_decay.T,
+        segment[:, None],
+        segment[None, :],
+    )
     restarts = first[tokens_here - 1] >= row_start
     tail_prefix = prefix[tokens_here - 1]
     base = jnp.zeros(states.shape[1:], states.dtype)
     for owner in range(states.shape[0]):
         base = jnp.where(tail_prefix == owner, states[owner], base)
-    map_half = carry_map.astype(jnp.bfloat16)
     fresh = jnp.einsum("hvj,hjk->hvk", base, map_half, preferred_element_type=jnp.float32)
     into_state = chain(
         jnp.where(restarts, 0, map_half).astype(jnp.bfloat16),
@@ -293,23 +367,16 @@
     owner_ids = jnp.arange(states.shape[0], dtype=jnp.int32)
     select = (prefix[None, :] == owner_ids[:, None]) & ~carried[None, :]
     select = jnp.concatenate([select, carried[None, :]], axis=0)
-    weight_vec = reach.astype(jnp.bfloat16)
-    core = local_out
-    for owner in range(states.shape[0] + 1):
-        held = states[owner] if owner < states.shape[0] else into_state
-        core = core + jnp.einsum(
-            "hik,hvk->hiv",
-            jnp.where(select[owner][None, :, None], weight_vec, 0),
-            held,
-            preferred_element_type=jnp.float32,
-        )
-    core_rows = jnp.transpose(core, (1, 0, 2))
-    normed = core_rows * lax.rsqrt(jnp.mean(core_rows * core_rows, axis=-1, keepdims=True) + 1e-06)
-    gate_rows = dn_gate.reshape(tokens_here, value_heads, DV).astype(jnp.float32)
-    dn_out = (
-        (normed * dn_norm_gain * jax.nn.silu(gate_rows))
-        .reshape(tokens_here, value_heads * DV)
-        .astype(jnp.bfloat16)
+    dn_out = whole_call(
+        finish_kernel,
+        jax.ShapeDtypeStruct((tokens_here, value_heads * DV), jnp.bfloat16),
+        local_out,
+        reach,
+        states,
+        into_state,
+        select.astype(jnp.float32).T,
+        dn_gate,
+        dn_norm_gain[None, :],
     )
     query_rot = rotate(
         at_query.reshape(tokens_here, query_heads, HD).astype(jnp.float32), cosines, sines, ROT

time: 94.6 us -> 79.1 us (0.84)
  matrix products: 24.4 us -> 4.81 us
  other arithmetic: 21 us -> 12.5 us
  Pallas kernels: 15.9 us -> 24.1 us
  starting transfers between devices: 8.88 us -> 16 us
  local copies, waits for them, and re-layouts: 19.7 us -> 16.4 us
  waiting for transfers between devices: 0.02 us -> 1.11 us
    dot_general x23 -> x0, matrix products: 22 us -> none  [the longest x6 4.08 us: unit_lower_inverse(): jnp.einsum('hij,hjk->hik', inverse, half, precision=HIGH)]
    pallas_call x0 -> x2, Pallas kernels: none -> 7.46 us  [whole_call(): pl.pallas_call(kernel, out_shape=shapes, in_specs=[space] * len(arrays),...]
    ppermute x6, starting transfers between devices: 8.88 us -> 16 us  [gathered(): lax.ppermute(x, 'context', [(i, (i + step) % size) for i in range(size)])]
    not x1, other arithmetic: 1.78 us -> 0.04 us  [shards(): select = (prefix[None, :] == owner_ids[:, None]) & ~carried[None, :]]
    convert_element_type x3 -> x0, local copies, waits for them, and re-layouts: 1.25 us -> none  [the longest x1 1.08 us: shards(): dn_gate.reshape(tokens_here, value_heads, DV).astype(jnp.float32)]
    dot_general x1, matrix products: 0.64 us -> 1.84 us  [absorb(): jnp.einsum('thd,nd->thn', queries, search_handles, preferred_element_type...]
    dot_general x1, matrix products: 0.77 us -> 1.95 us  [absorb(): jnp.einsum('thn,nd->thd', weights.astype(jnp.bfloat16), values, preferred...]
    slice x1, local copies, waits for them, and re-layouts: 0.62 us -> 1.77 us  [shards(): both[:, 1].reshape(-1, HD)]
  transfers between devices with their start and end apart: 6 -> 6, of which waited for: 0 -> 1; matrix products, arithmetic and copies ran while one was open for 60% -> 17% of each run, Pallas kernels for 17% -> 31%
where the time goes in v3:
time: 79.1 us; the launch traced here: 78.6 us
  Pallas kernels  24.1 us (30%)
  local copies, waits for them, and re-layouts  16.4 us (21%)
  starting transfers between devices  16 us (20%)
  other arithmetic  12.5 us (16%)
  matrix products  4.81 us (6%)
  between operations  3.65 us (5%)
  waiting for transfers between devices  1.11 us (1%)
    pallas_call x1, Pallas kernels, chain(): pl.pallas_call(lambda *refs: chain_kernel(size, *refs), out_shape=jax.Sha...  16.7 us
    ppermute x6, starting transfers between devices, gathered(): lax.ppermute(x, 'context', [(i, (i + step) % size) for i in range(size)])  16 us
    pallas_call x2, Pallas kernels, whole_call(): pl.pallas_call(kernel, out_shape=shapes, in_specs=[space] * len(arrays),...  7.46 us
    another operation x2, other arithmetic, gathered(): return (jnp.stack(turned), (me - jnp.arange(size, dtype=jnp.int32)) % size)  4.15 us
    slice x2, local copies, waits for them, and re-layouts, shards(): both[:, 0].reshape(-1, HD)  3.28 us
    another operation x3, other arithmetic  2.74 us
    unnamed x33, local copies, waits for them, and re-layouts  2.58 us
    dot_general x1, matrix products, absorb(): jnp.einsum('thn,nd->thd', weights.astype(jnp.bfloat16), values, preferred...  1.95 us
  transfers between devices with their start and end apart: 6, of which 1 were waited for; matrix products, arithmetic and copies ran while one was open for 17% of the time, Pallas kernels for 31%

profile of v3, /device:TPU:28, one launch (start us, length us, event | category | flops | bytes accessed | tf_op | source)
XLA Modules:
  0.0 78.6 jit_solution(12692233627112379803)
XLA Ops:
  0.7 0.9 %constant_dynamic-slice_fusion.1 = (bf16[128,256]{1,0:T(8,128)(2,1)S(1)}, bf16[128,256]{1,0:T(8,128)(2,1)S(1)}) fusion(bf16[128,512]{1,0:T(8,128)(2,1)} %param.28, s32[]{:T(128)S(6)} %select_n.163, bf16[128,512]{1,0:T(8,128)(2,1)} %param.29), kind=kLoop, calls=%fused_computation.96 | loop fusion | bytes 262148 | tf_op jit(solution)/shard_map/dynamic_slice | solution.py:314
  1.8 0.9 %reduce-window.9 = s32[4,1]{0,1:T(1,128)S(1)} reduce-window(s32[4,1]{0,1:T(1,128)} %bitcast.104, s32[]{:T(128)} %constant.129.clone.1), window={size=4x1 pad=3_0x0_0}, to_apply=%region_0.0 | reduce-window | flops 12 | bytes 36 | tf_op jit(solution)/shard_map/reduce-window.4
  2.6 0.7 bitcast_subtract_fusion
  3.4 0.9 %constant_dynamic-slice_fusion = (bf16[2,64,256]{2,1,0:T(8,128)(2,1)S(1)}, bf16[2,64,256]{2,1,0:T(8,128)(2,1)S(1)}) fusion(bf16[2,64,512]{2,1,0:T(8,128)(2,1)} %param.31, s32[]{:T(128)S(6)} %select_n.163, bf16[2,64,512]{2,1,0:T(8,128)(2,1)} %param.30), kind=kLoop, calls=%fused_computation.95 | loop fusion | bytes 262148 | tf_op jit(solution)/shard_map/dynamic_slice | solution.py:322
  4.4 0.1 copy.125
  4.5 0.1 copy.132
  4.7 0.8 select_reduce_fusion.1
  5.4 0.2 fusion.25
  5.7 0.8 reshape.500
  6.5 0.2 collective-permute-start.3
  6.7 1.7 %collective-permute-start.4 = (bf16[2,256,256]{1,0,2:T(2,128)(2,1)}, bf16[2,256,256]{1,0,2:T(2,128)(2,1)}, u32[]{:S(2)}, u32[]{:S(2)}) collective-permute-start(bf16[2,256,256]{1,0,2:T(2,128)(2,1)} %reshape.500), channel_id=1, source_target_pairs={{0,8},{4,12},{8,0},{12,4},{1,9},{5,13},{9,1},{13,5},{2,10},{6,14},... | collective-permute-start | bytes 786440 | tf_op jit(solution)/shard_map/ppermute | solution.py:90
  8.4 2.5 %collective-permute-start = (bf16[2,8,32,128]{3,2,1,0:T(8,128)(2,1)}, bf16[2,8,32,128]{3,2,1,0:T(8,128)(2,1)}, u32[]{:S(2)}, u32[]{:S(2)}) collective-permute-start(bf16[2,8,32,128]{3,2,1,0:T(8,128)(2,1)} %param.25), channel_id=1, source_target_pairs={{0,4},{4,8},{8,12},{12,0},{1,5},{5,9},{9,13},{13,1},{2,6},{6,10},{... | collective-permute-start | bytes 393224 | tf_op jit(solution)/shard_map/ppermute | solution.py:90
  10.8 0.8 collective-permute-start.2
  11.6 0.1 fusion.19
  11.8 0.6 fusion.51
  13.2 0.7 copy.119
  13.9 0.7 copy.120
  14.7 0.2 copy.117
  14.8 0.2 copy.118
  15.2 0.2 copy.128
  15.4 1.0 %add_divide_fusion = f32[128,1024]{0,1:T(8,128)} fusion(bf16[128,1024]{0,1:T(8,128)(2,1)S(1)} %copy.128), kind=kLoop, calls=%fused_computation.18 | loop fusion | flops 524288 | bytes 786432 | tf_op jit(solution)/shard_map/div | solution.py:412
  17.5 0.3 compare_and_fusion.1
  17.8 0.3 compare_and_fusion
  18.2 0.2 pad_add_fusion
  18.4 6.0 %shard_map.185 = (f32[8,128,128]{2,1,0:T(8,128)S(1)}, bf16[8,128,128]{2,1,0:T(8,128)(2,1)S(1)}, bf16[8,128,128]{2,1,0:T(8,128)(2,1)S(1)}, f32[8,128,128]{2,1,0:T(8,128)S(1)}) custom-call(bf16[128,512]{1,0:T(8,128)(2,1)S(1)} %copy-done.3, bf16[128,512]{1,0:T(8,128)(2,1)S(1)} %copy-done.4, bf16[128,1024]{1,0:T(8,128)(2,1)S(1)} %copy-done.2, ...), custom_call_target="tpu_custom_call" | custom-call | tf_op jit(solution)/shard_map/pallas_call | solution.py:213
  24.4 0.7 broadcast_select_fusion.refs_0_
  25.1 1.7 %subtract_convert_fusion = (bf16[128,4,32]{2,0,1:T(8,128)(2,1)}, bf16[128,4,32]{2,0,1:T(8,128)(2,1)}) fusion(f32[128,4,256]{2,0,1:T(8,128)S(1)} %convert_element_type.50, f32[128,32]{1,0:T(8,128)} %copy.120, f32[128,32]{1,0:T(8,128)} %copy.119), kind=kLoop, calls=%fused_computation.31 | loop fusion | flops 131072 | bytes 229376 | tf_op jit(solution)/shard_map/convert.7
  26.9 0.9 %slice.66 = bf16[128,4,192]{2,0,1:T(8,128)(2,1)} slice(bf16[128,4,256]{2,0,1:T(8,128)(2,1)S(1)} %copy.118), slice={[0:128], [0:4], [64:256]} | slice | bytes 393216 | tf_op jit(solution)/shard_map/slice | solution.py:248
  27.8 0.6 slice.47
  28.4 1.0 %copy.129 = f32[128,4,256]{2,0,1:T(8,128)} copy(f32[128,4,256]{0,2,1:T(8,128)S(1)} %bitcast.89) | data formatting | bytes 1048576 | tf_op jit(solution)/shard_map/div | solution.py:412
  30.9 10.8 %collective-permute-start.5 = (bf16[2,256,256]{1,0,2:T(2,128)(2,1)}, bf16[2,256,256]{1,0,2:T(2,128)(2,1)}, u32[]{:S(2)}, u32[]{:S(2)}) collective-permute-start(bf16[2,256,256]{1,0,2:T(2,128)(2,1)} %reshape.500), channel_id=1, source_target_pairs={{0,12},{4,0},{8,4},{12,8},{1,13},{5,1},{9,5},{13,9},{2,14},{6,2},{... | collective-permute-start | bytes 786440 | tf_op jit(solution)/shard_map/ppermute | solution.py:90
  41.7 1.1 %collective-permute-done.1 = bf16[2,8,32,128]{3,2,1,0:T(8,128)(2,1)} collective-permute-done((bf16[2,8,32,128]{3,2,1,0:T(8,128)(2,1)}, bf16[2,8,32,128]{3,2,1,0:T(8,128)(2,1)}, u32[]{:S(2)}, u32[]{:S(2)}) %collective-permute-start.1) | collective-permute-done | bytes 131104 | tf_op jit(solution)/shard_map/ppermute | solution.py:90
  42.8 1.2 %pad_maximum_fusion.1 = bf16[4,2,8,32,128]{4,3,2,1,0:T(8,128)(2,1)S(1)} fusion(bf16[1,2,8,32,128]{4,3,2,1,0:T(8,128)(2,1)} %bitcast.9, bf16[1,2,8,32,128]{4,3,2,1,0:T(8,128)(2,1)} %bitcast.8, bf16[1,2,8,32,128]{4,3,2,1,0:T(8,128)(2,1)} %bitcast.7, bf16[1,2,8,32,128]{4,3,2,1,0:T(8,128)(2,1)} %bitcast.6), kind=kLoop, calls=%fused_computation.17 | loop fusion | flops 786432 | bytes 1048576 | tf_op jit(solution)/shard_map/stack | solution.py:93
  44.0 0.6 gather_fusion
  44.6 0.1 select_bitcast_fusion
  44.9 1.0 %fusion.4.refs_1_ = f32[8,128,128]{2,1,0:T(8,128)} fusion(f32[8,128,128]{2,1,0:T(8,128)S(1)} %get-tuple-element.9, bf16[8,128,128]{2,1,0:T(8,128)(2,1)S(1)} %bitcast.92, bf16[8,128,128]{2,1,0:T(8,128)(2,1)S(1)} %get-tuple-element.8, pred[]{:T(512)S(6)} %ge.11), kind=kOutput, calls=%fused_computation.9 | convolution fusion | flops 33816576 | bytes 1572865 | tf_op jit(solution)/shard_map/hvj,hjk->hvk/dot_general | solution.py:360
  45.9 16.7 %shard_map.186.into_ref = bf16[8,128,128]{2,1,0:T(8,128)(2,1)} custom-call(bf16[8,128,128]{2,1,0:T(8,128)(2,1)} %broadcast_select_fusion.refs_0_, f32[8,128,128]{2,1,0:T(8,128)} %fusion.4.refs_1_), custom_call_target="tpu_custom_call" | custom-call | tf_op jit(solution)/shard_map/pallas_call | solution.py:73
  62.6 0.9 %copy-done = bf16[8,128,128]{2,1,0:T(8,128)(2,1)S(1)} copy-done((bf16[8,128,128]{2,1,0:T(8,128)(2,1)S(1)}, bf16[8,128,128]{2,1,0:T(8,128)(2,1)}, u32[]{:S(2)}) %copy-start) | copy-done | bytes 262168
  63.5 1.5 %shard_map.187 = bf16[128,1024]{1,0:T(8,128)(2,1)} custom-call(f32[8,128,128]{2,1,0:T(8,128)S(1)} %get-tuple-element.6.local_ref, bf16[8,128,128]{2,1,0:T(8,128)(2,1)S(1)} %get-tuple-element.7.reach_ref, bf16[2,8,128,128]{3,2,1,0:T(8,128)(2,1)S(1)} %bitcast.84, bf16[8,128,128]{2,1,0:T(8,128)(2,1)S(1)} %copy-done, f32[128,3]{1,0:T(8,128)S(1)} %bitcast.85, ...), custom_call_target="tpu_custom_call" | custom-call | tf_op jit(solution)/shard_map/pallas_call | solution.py:213
  65.0 3.0 %pad_maximum_fusion = bf16[4,2,256,256]{2,1,3,0:T(2,128)(2,1)S(1)} fusion(bf16[1,2,256,256]{2,1,3,0:T(2,128)(2,1)} %bitcast.32, bf16[1,2,256,256]{2,1,3,0:T(2,128)(2,1)} %bitcast.31, bf16[1,2,256,256]{2,1,3,0:T(2,128)(2,1)} %bitcast.30, bf16[1,2,256,256]{2,1,3,0:T(2,128)(2,1)S(1)} %stack_reshape.3), kind=kLoop, calls=%fused_computation.12 | loop fusion | flops 1572864 | bytes 2097152 | tf_op jit(solution)/shard_map/stack | solution.py:93
  68.0 1.5 %fusion.50 = (bf16[4,1,256,256]{2,1,3,0:T(2,128)(2,1)S(1)}, bf16[4,1,256,256]{2,1,3,0:T(2,128)(2,1)S(1)}) fusion(bf16[4,2,256,256]{2,1,3,0:T(2,128)(2,1)S(1)} %pad_maximum_fusion), kind=kLoop, calls=%fused_computation.124 | loop fusion | bytes 2097152 | tf_op jit(solution)/shard_map/slice | solution.py:406
  69.5 1.8 %copy.126 = bf16[4,1,256,256]{3,2,0,1:T(8,128)(2,1)} copy(bf16[4,1,256,256]{2,1,3,0:T(2,128)(2,1)S(1)} %get-tuple-element.25) | data formatting | bytes 1048576 | tf_op jit(solution)/shard_map/slice | solution.py:406
  71.3 1.8 %fusion = (f32[128,4]{0,1:T(4,128)S(1)}, f32[128,4,1024]{2,0,1:T(8,128)S(1)}) fusion(pred[128,1024]{1,0:T(8,128)(4,1)S(1)} %bitcast.95, bf16[1024,256,1]{1,0,2:T(8,128)(2,1)} %bitcast.94, bf16[128,4,192]{2,0,1:T(8,128)(2,1)} %slice.66, bf16[128,4,32]{2,0,1:T(8,128)(2,1)} %get-tuple-element.28, bf16[128,4,32]{2,0,1:T(8,128)(2,1)S(1)} %copy-done.11), kind=kOutput, calls=%fused_computation.3 | convolution fusion | flops 270794240 | bytes 3016704 | tf_op jit(solution)/shard_map/thd,nd->thn/dot_general | solution.py:268
  73.2 0.7 fusion.1
  73.9 1.8 %copy.127 = bf16[4,1,256,256]{3,2,0,1:T(8,128)(2,1)} copy(bf16[4,1,256,256]{2,1,3,0:T(2,128)(2,1)S(1)} %get-tuple-element.26) | data formatting | bytes 1048576 | tf_op jit(solution)/shard_map/slice | solution.py:406
  75.6 1.9 %fusion.6 = bf16[128,4,256]{2,0,1:T(8,128)(2,1)S(1)} fusion(f32[128,4,256]{2,0,1:T(8,128)} %copy.129, bf16[1024,256,1]{1,0,2:T(8,128)(2,1)} %bitcast.93, f32[128,4,1024]{2,0,1:T(8,128)S(1)} %get-tuple-element.45, f32[128,4]{0,1:T(4,128)S(1)} %broadcast_maximum_fusion, pred[128,1024]{1,0:T(8,128)(4,1)S(1)} %bitcast.97, f32[128,4]{0,1:T(4,128)S(1)} %get-tuple-element.32, ...), kind=kOutput, calls=%fused_computation.11 | convolution fusion | flops 271581184 | bytes 3545088 | tf_op jit(solution)/shard_map/thn,nd->thd/dot_general | solution.py:277
  77.6 0.2 copy.130
  77.8 0.9 %copy.131 = bf16[128,1024]{1,0:T(8,128)(2,1)} copy(bf16[128,1024]{0,1:T(8,128)(2,1)S(1)} %bitcast.90) | data formatting | bytes 524288
  (69 shorter events, 1.7 us)
Async XLA Ops:
  0.6 14.0 %copy-start.9 = (bf16[128,1024]{1,0:T(8,128)(2,1)S(1)}, bf16[128,1024]{1,0:T(8,128)(2,1)}, u32[]{:S(2)}) copy-start(bf16[128,1024]{1,0:T(8,128)(2,1)} %param.26) | copy-start | bytes 786436
  1.7 13.5 %copy-start.10 = (bf16[128,1024]{1,0:T(8,128)(2,1)S(1)}, bf16[128,1024]{1,0:T(8,128)(2,1)}, u32[]{:S(2)}) copy-start(bf16[128,1024]{1,0:T(8,128)(2,1)} %param.27) | copy-start | bytes 786436
  5.6 10.8 %copy-start.5 = (f32[128,8]{0,1:T(8,128)S(1)}, f32[128,8]{0,1:T(8,128)}, u32[]{:S(2)}) copy-start(f32[128,8]{0,1:T(8,128)} %param.22) | copy-start | bytes 12292
  5.6 10.9 %copy-start.6 = (f32[128,8]{0,1:T(8,128)S(1)}, f32[128,8]{0,1:T(8,128)}, u32[]{:S(2)}) copy-start(f32[128,8]{0,1:T(8,128)} %param.23) | copy-start | bytes 12292
  5.7 11.7 %copy-start.12 = (s32[8]{0:T(128)S(1)}, s32[8]{0:T(128)}, u32[]{:S(2)}) copy-start(s32[8]{0:T(128)} %param.35) | copy-start | bytes 100
  6.4 11.9 %copy-start.2 = (bf16[128,1024]{1,0:T(8,128)(2,1)S(1)}, bf16[128,1024]{1,0:T(8,128)(2,1)}, u32[]{:S(2)}) copy-start(bf16[128,1024]{1,0:T(8,128)(2,1)} %value_ref.1) | copy-start | bytes 786436
  6.4 11.9 %copy-start.3 = (bf16[128,512]{1,0:T(8,128)(2,1)S(1)}, bf16[128,512]{1,0:T(8,128)(2,1)}, u32[]{:S(2)}) copy-start(bf16[128,512]{1,0:T(8,128)(2,1)} %query_ref.1) | copy-start | bytes 393220
  6.5 11.9 %copy-start.4 = (bf16[128,512]{1,0:T(8,128)(2,1)S(1)}, bf16[128,512]{1,0:T(8,128)(2,1)}, u32[]{:S(2)}) copy-start(bf16[128,512]{1,0:T(8,128)(2,1)} %key_ref.1) | copy-start | bytes 393220
  6.5 58.6 %collective-permute-start.3 = (bf16[2,256,256]{1,0,2:T(2,128)(2,1)}, bf16[2,256,256]{1,0,2:T(2,128)(2,1)}, u32[]{:S(2)}, u32[]{:S(2)}) collective-permute-start(bf16[2,256,256]{1,0,2:T(2,128)(2,1)} %reshape.500), channel_id=1, source_target_pairs={{0,4},{4,8},{8,12},{12,0},{1,5},{5,9},{9,13},{13,1},{2,6},{6,10},{... | collective-permute-start | bytes 786440 | tf_op jit(solution)/shard_map/ppermute | solution.py:90
  6.7 58.3 %collective-permute-start.4 = (bf16[2,256,256]{1,0,2:T(2,128)(2,1)}, bf16[2,256,256]{1,0,2:T(2,128)(2,1)}, u32[]{:S(2)}, u32[]{:S(2)}) collective-permute-start(bf16[2,256,256]{1,0,2:T(2,128)(2,1)} %reshape.500), channel_id=1, source_target_pairs={{0,8},{4,12},{8,0},{12,4},{1,9},{5,13},{9,1},{13,5},{2,10},{6,14},... | collective-permute-start | bytes 786440 | tf_op jit(solution)/shard_map/ppermute | solution.py:90
  8.4 22.5 %collective-permute-start = (bf16[2,8,32,128]{3,2,1,0:T(8,128)(2,1)}, bf16[2,8,32,128]{3,2,1,0:T(8,128)(2,1)}, u32[]{:S(2)}, u32[]{:S(2)}) collective-permute-start(bf16[2,8,32,128]{3,2,1,0:T(8,128)(2,1)} %param.25), channel_id=1, source_target_pairs={{0,4},{4,8},{8,12},{12,0},{1,5},{5,9},{9,13},{13,1},{2,6},{6,10},{... | collective-permute-start | bytes 393224 | tf_op jit(solution)/shard_map/ppermute | solution.py:90
  10.8 31.9 %collective-permute-start.1 = (bf16[2,8,32,128]{3,2,1,0:T(8,128)(2,1)}, bf16[2,8,32,128]{3,2,1,0:T(8,128)(2,1)}, u32[]{:S(2)}, u32[]{:S(2)}) collective-permute-start(bf16[2,8,32,128]{3,2,1,0:T(8,128)(2,1)} %param.25), channel_id=1, source_target_pairs={{0,8},{4,12},{8,0},{12,4},{1,9},{5,13},{9,1},{13,5},{2,10},{6,14},... | collective-permute-start | bytes 393224 | tf_op jit(solution)/shard_map/ppermute | solution.py:90
  10.8 31.9 %collective-permute-start.2 = (bf16[2,8,32,128]{3,2,1,0:T(8,128)(2,1)}, bf16[2,8,32,128]{3,2,1,0:T(8,128)(2,1)}, u32[]{:S(2)}, u32[]{:S(2)}) collective-permute-start(bf16[2,8,32,128]{3,2,1,0:T(8,128)(2,1)} %param.25), channel_id=1, source_target_pairs={{0,12},{4,0},{8,4},{12,8},{1,13},{5,1},{9,5},{13,9},{2,14},{6,2},{... | collective-permute-start | bytes 393224 | tf_op jit(solution)/shard_map/ppermute | solution.py:90
  24.4 4.1 %copy-start.8 = (f32[128,1024]{0,1:T(8,128)S(1)}, f32[128,1024]{0,1:T(8,128)}, u32[]{:S(2)}) copy-start(f32[128,1024]{0,1:T(8,128)} %add_divide_fusion) | copy-start | bytes 1572868
  30.9 34.2 %collective-permute-start.5 = (bf16[2,256,256]{1,0,2:T(2,128)(2,1)}, bf16[2,256,256]{1,0,2:T(2,128)(2,1)}, u32[]{:S(2)}, u32[]{:S(2)}) collective-permute-start(bf16[2,256,256]{1,0,2:T(2,128)(2,1)} %reshape.500), channel_id=1, source_target_pairs={{0,12},{4,0},{8,4},{12,8},{1,13},{5,1},{9,5},{13,9},{2,14},{6,2},{... | collective-permute-start | bytes 786440 | tf_op jit(solution)/shard_map/ppermute | solution.py:90
  44.8 17.8 %copy-start.1 = (bf16[128,1024]{1,0:T(8,128)(2,1)S(1)}, bf16[128,1024]{1,0:T(8,128)(2,1)}, u32[]{:S(2)}) copy-start(bf16[128,1024]{1,0:T(8,128)(2,1)} %gate_ref.1) | copy-start | bytes 786436
  44.8 17.8 %copy-start.7 = (f32[128]{0:T(128)S(1)}, f32[128]{0:T(128)}, u32[]{:S(2)}) copy-start(f32[128]{0:T(128)} %param.24) | copy-start | bytes 1540
  62.6 1.0 %copy-start = (bf16[8,128,128]{2,1,0:T(8,128)(2,1)S(1)}, bf16[8,128,128]{2,1,0:T(8,128)(2,1)}, u32[]{:S(2)}) copy-start(bf16[8,128,128]{2,1,0:T(8,128)(2,1)} %shard_map.186.into_ref) | copy-start | bytes 786436
  68.0 3.3 %copy-start.11 = (bf16[128,4,32]{2,0,1:T(8,128)(2,1)S(1)}, bf16[128,4,32]{2,0,1:T(8,128)(2,1)}, u32[]{:S(2)}) copy-start(bf16[128,4,32]{2,0,1:T(8,128)(2,1)} %get-tuple-element.27) | copy-start | bytes 98308

commit v4 on v3

--- a/solution.py
+++ b/solution.py
@@ -85,12 +85,13 @@
     )(carry_map, carry_add)
 
 
-def gathered(x, size, me):
-    turned = [x] + [
-        lax.ppermute(x, "context", [(i, (i + step) % size) for i in range(size)])
-        for step in range(1, size)
+def from_others(x, axis, size, span):
+    return [
+        lax.ppermute(
+            x, axis, [(i, i // span * span + (i + step) % span) for i in range(size)]
+        )
+        for step in range(1, span)
     ]
-    return jnp.stack(turned), (me - jnp.arange(size, dtype=jnp.int32)) % size
 
 
 def halves(x):
@@ -208,6 +209,59 @@
         ).astype(jnp.bfloat16)
 
 
+def attend_kernel(
+    query_ref, cos_ref, sin_ref, gate_ref, row_ref, code_ref, place_ref, own_ref, *rest
+):
+    pieces, out_ref = [own_ref] + list(rest[:-1]), rest[-1]
+    tokens = query_ref.shape[0]
+    cosines, sines = cos_ref[...], sin_ref[...]
+    lane = lax.broadcasted_iota(jnp.int32, (tokens, 128), 1)
+    old_code, limit = row_ref[:, 0:1], row_ref[:, 1:2]
+    new_code, own_row = row_ref[:, 2:3], row_ref[:, 3:4]
+    keys, values, seen, at = [], [], [], 0
+    for ref in pieces:
+        if len(ref.shape) == 3:
+            keys.append(ref[0])
+            values.append(ref[1])
+        else:
+            keys.append(ref[:, 0].reshape(-1, HD))
+            values.append(ref[:, 1].reshape(-1, HD))
+        count = keys[-1].shape[0]
+        code, place = code_ref[:, at : at + count], place_ref[:, at : at + count]
+        at += count
+        seen.append(
+            ((code == old_code) & (place < limit)) | ((code == new_code) & (place <= own_row))
+        )
+    for h in range(query_ref.shape[1] // HD):
+        front = query_ref[:, h * HD : h * HD + 128].astype(jnp.float32)
+        swapped = jnp.where(
+            lane < ROT // 2, pltpu.roll(front, 128 - ROT // 2, 1), pltpu.roll(front, ROT // 2, 1)
+        )
+        query = jnp.concatenate(
+            [
+                (front * cosines + swapped * sines).astype(jnp.bfloat16),
+                query_ref[:, h * HD + 128 : (h + 1) * HD],
+            ],
+            axis=1,
+        )
+        scores = [
+            jnp.where(see, dot1(query, key, ((1,), (1,))) * HD ** (-0.5), NEG_LARGE)
+            for see, key in zip(seen, keys)
+        ]
+        peak = jnp.max(scores[0], axis=1, keepdims=True)
+        for score in scores[1:]:
+            peak = jnp.maximum(peak, jnp.max(score, axis=1, keepdims=True))
+        total, summed = 0.0, 0.0
+        for score, see, value in zip(scores, seen, values):
+            weight = jnp.where(see, jnp.exp(score - peak), 0.0)
+            total = total + jnp.sum(weight, axis=1, keepdims=True)
+            summed = summed + dot1(weight.astype(jnp.bfloat16), value)
+        gate = gate_ref[:, h * HD : (h + 1) * HD].astype(jnp.float32)
+        out_ref[:, h * HD : (h + 1) * HD] = (
+            summed / total * jax.nn.sigmoid(gate)
+        ).astype(jnp.bfloat16)
+
+
 def whole_call(kernel, shapes, *arrays):
     space = pl.BlockSpec(memory_space=pltpu.VMEM)
     return pl.pallas_call(
@@ -261,23 +315,6 @@
     prefix = jnp.sum(choose * req_prefix[None, :], axis=1)
     offset = jnp.sum(choose * req_offset[None, :], axis=1)
     return (segment, first, prefix, offset, offset + rows - first)
-
-
-def absorb(state, queries, search_handles, values, visible):
-    peak, total, summed = state
-    scores = jnp.einsum(
-        "thd,nd->thn", queries, search_handles, preferred_element_type=jnp.float32
-    ) * search_handles.shape[-1] ** (-0.5)
-    seen = visible[:, None, :]
-    scores = jnp.where(seen, scores, NEG_LARGE)
-    new_peak = jnp.maximum(peak, jnp.max(scores, axis=-1))
-    weights = jnp.where(seen, jnp.exp(scores - new_peak[..., None]), 0.0)
-    shrink = jnp.exp(peak - new_peak)
-    total = total * shrink + jnp.sum(weights, axis=-1)
-    summed = summed * shrink[..., None] + jnp.einsum(
-        "thn,nd->thd", weights.astype(jnp.bfloat16), values, preferred_element_type=jnp.float32
-    )
-    return (new_peak, total, summed)
 
 
 def shards(
@@ -320,18 +357,21 @@
     new_value = lax.dynamic_slice_in_dim(at_value, kv_head * HD, HD, 1)
     cached_key = lax.dynamic_slice_in_dim(prefix_key, kv_head * HD, HD, 2)
     cached_value = lax.dynamic_slice_in_dim(prefix_value, kv_head * HD, HD, 2)
-    states, origin = gathered(prefix_state, size, device)
-    states = jnp.take(states, origin, axis=0)
+    states = jnp.stack([prefix_state] + from_others(prefix_state, "context", size, size))
+    states = jnp.take(states, (device - jnp.arange(size, dtype=jnp.int32)) % size, axis=0)
     states = jnp.moveaxis(states, 0, 2)
     states = states.reshape(states.shape[:2] + (-1, DK))
     slots_here = cached_key.shape[0]
-    both, origin = gathered(
-        jnp.concatenate(
-            [cached_key.reshape(-1, HD), new_key, cached_value.reshape(-1, HD), new_value]
-        ).reshape(2, -1, HD),
-        size,
-        device,
-    )
+    own_block = jnp.concatenate(
+        [cached_key.reshape(-1, HD), new_key, cached_value.reshape(-1, HD), new_value]
+    ).reshape(2, -1, HD)
+    block_rows = own_block.shape[1]
+    sharers = HQ // KVH // query_heads
+    share = block_rows // sharers
+    share_index = lax.axis_index("head") % sharers
+    mine = lax.dynamic_slice_in_dim(own_block, share_index * share, share, 1)
+    received = jnp.stack(from_others(mine, "context", size, size))
+    siblings = from_others(received, "head", lax.axis_size("head"), sharers)
     cached_rows = cached_key.shape[0] * cached_key.shape[1]
     square = (value_heads, DK, DK)
     local_out, reach, map_half, carry_add = whole_call(
@@ -378,40 +418,48 @@
         dn_gate,
         dn_norm_gain[None, :],
     )
-    query_rot = rotate(
-        at_query.reshape(tokens_here, query_heads, HD).astype(jnp.float32), cosines, sines, ROT
-    ).astype(jnp.bfloat16)
-    table_index = jnp.arange(block_table.shape[0], dtype=jnp.int32)
     blocks_per_prefix = block_table.shape[0] // prefix_state.shape[0]
-    state = (
-        jnp.full((tokens_here, query_heads), NEG_LARGE, jnp.float32),
-        jnp.zeros((tokens_here, query_heads), jnp.float32),
-        jnp.zeros((tokens_here, query_heads, HD), jnp.float32),
-    )
-    part = jnp.arange(cached_rows, dtype=jnp.int32)
     width = cached_key.shape[1]
-    slots = (origin[:, None] * slots_here + part[None, :] // width).reshape(-1)
+    others = (device - 1 - jnp.arange(size - 1, dtype=jnp.int32)) % size
+    origins = [jnp.full((block_rows,), device, jnp.int32)]
+    parts = [jnp.arange(block_rows, dtype=jnp.int32)]
+    for step in range(sharers):
+        origins.append(jnp.repeat(others, share))
+        parts.append(
+            (share_index - step) % sharers * share
+            + jnp.tile(jnp.arange(share, dtype=jnp.int32), size - 1)
+        )
+    origin, part = jnp.concatenate(origins), jnp.concatenate(parts)
+    slot = origin * slots_here + part // width
     entry = jnp.sum(
-        jnp.where(block_table[None, :] == slots[:, None], table_index[None, :], 0), axis=1
-    ).reshape(size, cached_rows)
-    owner = entry // blocks_per_prefix
-    where_in = entry % blocks_per_prefix * width + part[None, :] % width
-    key_rows = origin[:, None] * tokens_here + jnp.arange(tokens_here, dtype=jnp.int32)[None, :]
-    key_segment = row_layout(key_rows.reshape(-1), req_len, req_prefix, req_offset)[0]
-    key_segment = key_segment.reshape(size, tokens_here)
-    old_seen = (owner[None] == prefix[:, None, None]) & (where_in[None] < offset[:, None, None])
-    new_seen = (key_segment[None] == segment[:, None, None]) & (key_rows[None] <= rows[:, None, None])
-    visible = jnp.concatenate([old_seen, new_seen], axis=2).reshape(tokens_here, -1)
-    state = absorb(
-        state, query_rot, both[:, 0].reshape(-1, HD), both[:, 1].reshape(-1, HD), visible
-    )
-    peak, total, summed = state
-    attention = summed / total[..., None]
-    gate_att = at_gate.reshape(tokens_here, query_heads, HD).astype(jnp.float32)
-    at_out = (
-        (attention * jax.nn.sigmoid(gate_att))
-        .reshape(tokens_here, query_heads * HD)
-        .astype(jnp.bfloat16)
+        jnp.where(
+            block_table[:, None] == slot[None, :],
+            jnp.arange(block_table.shape[0], dtype=jnp.int32)[:, None],
+            0,
+        ),
+        axis=0,
+    )
+    key_row = origin * tokens_here + part - cached_rows
+    starts = jnp.cumsum(req_len) - req_len
+    key_segment = jnp.sum((starts[:, None] <= key_row[None, :]).astype(jnp.int32), axis=0) - 1
+    old = part < cached_rows
+    prefixes = prefix_state.shape[0]
+    code = jnp.where(old, entry // blocks_per_prefix, prefixes + key_segment)
+    place = jnp.where(old, entry % blocks_per_prefix * width + part % width, key_row)
+    ones = jnp.ones((tokens_here, 128 - ROT), jnp.float32)
+    at_out = whole_call(
+        attend_kernel,
+        jax.ShapeDtypeStruct((tokens_here, query_heads * HD), jnp.bfloat16),
+        at_query,
+        jnp.concatenate([cosines, cosines, ones], axis=1),
+        jnp.concatenate([-sines, sines, 0.0 * ones], axis=1),
+        at_gate,
+        jnp.stack([prefix, offset, prefixes + segment, rows], axis=1),
+        code[None, :],
+        place[None, :],
+        own_block,
+        received,
+        *siblings,
     )
     return (dn_out, at_out)
 

time: 79.1 us -> 57.2 us (0.72)
  starting transfers between devices: 16 us -> 7.15 us
  local copies, waits for them, and re-layouts: 16.4 us -> 7.86 us
  other arithmetic: 12.5 us -> 4.49 us
  waiting for transfers between devices: 1.11 us -> 5.4 us
  matrix products: 4.81 us -> 1.01 us
  Pallas kernels: 24.1 us -> 27.2 us
    ppermute x6 -> x7, starting transfers between devices: 16 us -> 7.15 us  [from_others(): lax.ppermute(x, axis, [(i, i // span * span + (i + step) % span) for i in...]
    another operation x7 -> x5, other arithmetic: 6.9 us -> 1.48 us  [the longest x1 1.1 us: shards(): jnp.stack([prefix_state] + from_others(prefix_state, 'context', size, size))]
    slice x3 -> x0, local copies, waits for them, and re-layouts: 5.05 us -> none  [the longest x2 3.28 us: shards(): both[:, 0].reshape(-1, HD)]
    ppermute x6 -> x7, waiting for transfers between devices: 1.11 us -> 5.4 us  [from_others(): lax.ppermute(x, axis, [(i, i // span * span + (i + step) % span) for i in...]
    dot_general x2 -> x0, matrix products: 3.78 us -> none  [the longest x1 1.95 us: absorb(): jnp.einsum('thn,nd->thd', weights.astype(jnp.bfloat16), values, preferred...]
    pallas_call x2 -> x3, Pallas kernels: 7.46 us -> 10.6 us  [whole_call(): pl.pallas_call(kernel, out_shape=shapes, in_specs=[space] * len(arrays),...]
    mul x2 -> x1, local copies, waits for them, and re-layouts: 1.46 us -> 0.01 us  [shards(): 0.0 * ones]
    select_n x4, other arithmetic: 0.15 us -> 1.24 us  [the longest x2 1.17 us: shards(): jnp.take(states, (device - jnp.arange(size, dtype=jnp.int32)) % size, axi...]
  transfers between devices with their start and end apart: 6 -> 7, of which waited for: 1 -> 1; matrix products, arithmetic and copies ran while one was open for 17% -> 15% of each run, Pallas kernels for 31% -> 42%
where the time goes in v4:
time: 57.2 us; the launch traced here: 56.8 us
  Pallas kernels  27.2 us (48%)
  local copies, waits for them, and re-layouts  7.86 us (14%)
  starting transfers between devices  7.15 us (12%)
  waiting for transfers between devices  5.4 us (9%)
  other arithmetic  4.49 us (8%)
  between operations  3.73 us (7%)
  matrix products  1.01 us (2%)
    pallas_call x1, Pallas kernels, chain(): pl.pallas_call(lambda *refs: chain_kernel(size, *refs), out_shape=jax.Sha...  16.5 us
    pallas_call x3, Pallas kernels, whole_call(): pl.pallas_call(kernel, out_shape=shapes, in_specs=[space] * len(arrays),...  10.6 us
    ppermute x7, starting transfers between devices, from_others(): lax.ppermute(x, axis, [(i, i // span * span + (i + step) % span) for i in...  7.15 us
    ppermute x7, waiting for transfers between devices, from_others(): lax.ppermute(x, axis, [(i, i // span * span + (i + step) % span) for i in...  5.4 us
    unnamed x39, local copies, waits for them, and re-layouts  3.34 us
    gather x1, local copies, waits for them, and re-layouts, shards(): jnp.take(states, (device - jnp.arange(size, dtype=jnp.int32)) % size, axi...  1.4 us
    select_n x2, other arithmetic, shards(): jnp.take(states, (device - jnp.arange(size, dtype=jnp.int32)) % size, axi...  1.17 us
  transfers between devices with their start and end apart: 7, of which 1 were waited for; matrix products, arithmetic and copies ran while one was open for 15% of the time, Pallas kernels for 42%

profile of v4, /device:TPU:28, one launch (start us, length us, event | category | flops | bytes accessed | tf_op | source)
XLA Modules:
  0.0 56.8 jit_solution(13905486288676378755)
XLA Ops:
  0.7 0.9 %constant_dynamic-slice_fusion.1 = (bf16[128,256]{1,0:T(8,128)(2,1)S(1)}, bf16[128,256]{1,0:T(8,128)(2,1)S(1)}) fusion(bf16[128,512]{1,0:T(8,128)(2,1)} %param.29, s32[]{:T(128)S(6)} %select_n.200, bf16[128,512]{1,0:T(8,128)(2,1)} %param.28), kind=kLoop, calls=%fused_computation.93 | loop fusion | bytes 262148 | tf_op jit(solution)/shard_map/dynamic_slice | solution.py:357
  1.6 0.1 copy.78
  1.8 0.5 copy-done.16
  2.2 0.2 reduce-window.9
  2.4 0.1 convert_reduce_fusion.1
  2.5 0.1 copy-done.11
  2.6 0.1 copy-done.12
  2.7 0.1 copy.80
  2.8 0.1 copy.81
  2.9 0.1 copy.84
  3.1 0.6 %copy-done.13 = s32[4]{0:T(128)S(1)} copy-done((s32[4]{0:T(128)S(1)}, s32[4]{0:T(128)}, u32[]{:S(2)}) %copy-start.13) | copy-done | bytes 40
  3.7 0.0 copy-done.14
  3.7 0.1 select_reduce_fusion.1
  3.8 0.1 fusion.9
  4.0 0.1 copy.82
  4.2 0.3 collective-permute-start.3
  4.5 1.7 %collective-permute-start.4 = (bf16[2,128,256]{2,1,0:T(8,128)(2,1)S(1)}, bf16[2,128,256]{2,1,0:T(8,128)(2,1)S(1)}, u32[]{:S(2)}, u32[]{:S(2)}) collective-permute-start(bf16[2,128,256]{2,1,0:T(8,128)(2,1)S(1)} %constant_dynamic-slice_fusion), channel_id=1, source_target_pairs={{0,8},{4,12},{8,0},{12,4},{1,9},{5,13},{9,1},{13,5},{2,10},{6,14},... | collective-permute-start | bytes 393224 | tf_op jit(solution)/shard_map/ppermute | solution.py:90
  6.2 0.4 collective-permute-start.5
  6.6 3.4 %collective-permute-start = (bf16[2,8,32,128]{3,2,1,0:T(8,128)(2,1)S(1)}, bf16[2,8,32,128]{3,2,1,0:T(8,128)(2,1)}, u32[]{:S(2)}, u32[]{:S(2)}) collective-permute-start(bf16[2,8,32,128]{3,2,1,0:T(8,128)(2,1)S(1)} %copy-done.10), channel_id=1, source_target_pairs={{0,4},{4,8},{8,12},{12,0},{1,5},{5,9},{9,13},{13,1},{2,6},{6,10},{... | collective-permute-start | bytes 393224 | tf_op jit(solution)/shard_map/ppermute | solution.py:90
  10.1 0.3 fusion.4
  10.4 0.6 %fusion.36 = (s32[1]{0:T(128)}, s32[1]{0:T(128)}) fusion(s32[128]{0:T(128)S(1)} %get-tuple-element.11), kind=kLoop, calls=%fused_computation.119 | loop fusion | bytes 16 | tf_op jit(solution)/shard_map/slice | solution.py:406
  11.8 0.1 broadcast_bitcast_fusion
  11.9 0.1 convert_reduce_fusion
  12.0 0.1 pad.28.clone
  12.1 0.1 pad.31.clone
  12.2 0.1 copy.73.seg_ref
  12.3 0.1 copy.71.logit_ref
  12.4 0.1 copy.72.decay_ref
  13.2 0.1 select_reduce_fusion
  13.3 6.0 %shard_map.185 = (f32[8,128,128]{2,1,0:T(8,128)S(1)}, bf16[8,128,128]{2,1,0:T(8,128)(2,1)S(1)}, bf16[8,128,128]{2,1,0:T(8,128)(2,1)S(1)}, f32[8,128,128]{2,1,0:T(8,128)S(1)}) custom-call(bf16[128,512]{1,0:T(8,128)(2,1)S(1)} %copy-done.5, bf16[128,512]{1,0:T(8,128)(2,1)S(1)} %copy-done.6, bf16[128,1024]{1,0:T(8,128)(2,1)S(1)} %copy-done.2, ...), custom_call_target="tpu_custom_call" | custom-call | tf_op jit(solution)/shard_map/pallas_call | solution.py:267
  19.3 0.7 %broadcast_select_fusion.refs_0_ = bf16[8,128,128]{2,1,0:T(8,128)(2,1)} fusion(bf16[8,128,128]{2,1,0:T(8,128)(2,1)S(1)} %get-tuple-element.8, pred[]{:T(512)S(6)} %ge.11), kind=kLoop, calls=%fused_computation.9 | loop fusion | flops 131072 | bytes 524289 | tf_op jit(solution)/shard_map/jit(_where)/select_n | solution.py:402
  20.0 0.1 maximum_maximum_fusion
  20.2 0.1 compare_select_fusion.5
  20.3 1.3 %collective-permute-start.2 = (bf16[2,8,32,128]{3,2,1,0:T(8,128)(2,1)S(1)}, bf16[2,8,32,128]{3,2,1,0:T(8,128)(2,1)}, u32[]{:S(2)}, u32[]{:S(2)}) collective-permute-start(bf16[2,8,32,128]{3,2,1,0:T(8,128)(2,1)S(1)} %copy-done.10), channel_id=1, source_target_pairs={{0,12},{4,0},{8,4},{12,8},{1,13},{5,1},{9,5},{13,9},{2,14},{6,2},{... | collective-permute-start | bytes 393224 | tf_op jit(solution)/shard_map/ppermute | solution.py:90
  21.6 0.6 %slice.31 = s32[1]{0:T(128)} slice(s32[128]{0:T(128)S(1)} %get-tuple-element.12), slice={[127:128]} | slice | bytes 8 | tf_op jit(solution)/shard_map/slice | solution.py:396
  22.1 0.1 copy.83.row_ref
  23.5 0.1 copy.76
  23.7 0.1 collective-permute-start.6
  23.8 5.4 %collective-permute-done.1 = bf16[2,8,32,128]{3,2,1,0:T(8,128)(2,1)} collective-permute-done((bf16[2,8,32,128]{3,2,1,0:T(8,128)(2,1)S(1)}, bf16[2,8,32,128]{3,2,1,0:T(8,128)(2,1)}, u32[]{:S(2)}, u32[]{:S(2)}) %collective-permute-start.1) | collective-permute-done | bytes 131104 | tf_op jit(solution)/shard_map/ppermute | solution.py:90
  29.2 1.1 %pad_maximum_fusion = bf16[4,2,8,32,128]{4,3,2,1,0:T(8,128)(2,1)S(1)} fusion(bf16[1,2,8,32,128]{4,3,2,1,0:T(8,128)(2,1)} %bitcast.9, bf16[1,2,8,32,128]{4,3,2,1,0:T(8,128)(2,1)} %bitcast.8, bf16[1,2,8,32,128]{4,3,2,1,0:T(8,128)(2,1)} %bitcast.7, bf16[1,2,8,32,128]{4,3,2,1,0:T(8,128)(2,1)S(1)} %bitcast.83), kind=kLoop, calls=%fused_computation.3 | loop fusion | flops 786432 | bytes 1048576 | tf_op jit(solution)/shard_map/stack | solution.py:360
  30.3 1.4 %gather_fusion = bf16[4,2,8,32,128]{4,3,2,1,0:T(8,128)(2,1)} fusion(bf16[4,2,8,32,128]{4,3,2,1,0:T(8,128)(2,1)S(1)} %pad_maximum_fusion, s32[1024]{0:T(1024)S(1)} %pad_clamp_fusion), kind=kCustom, calls=%fused_computation | custom fusion | bytes 1048592 | tf_op jit(solution)/shard_map/jit(_take)/gather | solution.py:361
  31.7 1.2 %select_bitcast_fusion = bf16[2,8,4,32,128]{4,3,1,0,2:T(8,128)(2,1)S(1)} fusion(bf16[4,2,8,32,128]{4,3,2,1,0:T(8,128)(2,1)} %gather_fusion, pred[4]{0:T(512)(128)(4,1)S(1)} %compare_and_fusion.2), kind=kLoop, calls=%fused_computation.4 | loop fusion | flops 262144 | bytes 1048580 | tf_op jit(solution)/shard_map/jit(_take)/select_n | solution.py:361
  33.0 1.0 %fusion.refs_1_ = f32[8,128,128]{2,1,0:T(8,128)} fusion(f32[8,128,128]{2,1,0:T(8,128)S(1)} %get-tuple-element.9, bf16[8,128,128]{2,1,0:T(8,128)(2,1)S(1)} %bitcast.76, bf16[8,128,128]{2,1,0:T(8,128)(2,1)S(1)} %get-tuple-element.8, pred[]{:T(512)S(6)} %ge.11), kind=kOutput, calls=%fused_computation.2 | convolution fusion | flops 33816576 | bytes 1572865 | tf_op jit(solution)/shard_map/hvj,hjk->hvk/dot_general | solution.py:400
  34.0 16.5 %shard_map.186.into_ref = bf16[8,128,128]{2,1,0:T(8,128)(2,1)} custom-call(bf16[8,128,128]{2,1,0:T(8,128)(2,1)} %broadcast_select_fusion.refs_0_, f32[8,128,128]{2,1,0:T(8,128)} %fusion.refs_1_), custom_call_target="tpu_custom_call" | custom-call | tf_op jit(solution)/shard_map/pallas_call | solution.py:73
  50.6 0.6 %copy-done.9 = f32[128]{0:T(128)S(1)} copy-done((f32[128]{0:T(128)S(1)}, f32[128]{0:T(128)}, u32[]{:S(2)}) %copy-start.9) | copy-done | bytes 536
  51.2 0.9 %copy-done = bf16[8,128,128]{2,1,0:T(8,128)(2,1)S(1)} copy-done((bf16[8,128,128]{2,1,0:T(8,128)(2,1)S(1)}, bf16[8,128,128]{2,1,0:T(8,128)(2,1)}, u32[]{:S(2)}) %copy-start) | copy-done | bytes 262168
  52.2 1.5 %shard_map.187 = bf16[128,1024]{1,0:T(8,128)(2,1)} custom-call(f32[8,128,128]{2,1,0:T(8,128)S(1)} %get-tuple-element.6.local_ref, bf16[8,128,128]{2,1,0:T(8,128)(2,1)S(1)} %get-tuple-element.7.reach_ref, bf16[2,8,128,128]{3,2,1,0:T(8,128)(2,1)S(1)} %bitcast.69, bf16[8,128,128]{2,1,0:T(8,128)(2,1)S(1)} %copy-done, f32[128,3]{1,0:T(8,128)S(1)} %bitcast.72, ...), custom_call_target="tpu_custom_call" | custom-call | tf_op jit(solution)/shard_map/pallas_call | solution.py:267
  53.7 3.1 %shard_map.188 = bf16[128,1024]{1,0:T(8,128)(2,1)} custom-call(bf16[128,1024]{1,0:T(8,128)(2,1)S(1)} %copy-done.3, f32[128,128]{1,0:T(8,128)S(1)} %get-tuple-element.31.cos_ref, f32[128,128]{1,0:T(8,128)S(1)} %get-tuple-element.32.sin_ref, bf16[128,1024]{1,0:T(8,128)(2,1)S(1)} %copy-done.4, s32[128,4]{1,0:T(8,128)S(1)} %copy.83.row_ref, ...), custom_call_target="tpu_custom_call" | custom-call | tf_op jit(solution)/shard_map/pallas_call | solution.py:267
  (71 shorter events, 0.6 us)
Async XLA Ops:
  1.6 0.7 %copy-start.16 = (s32[4]{0:T(128)S(1)}, s32[4]{0:T(128)}, u32[]{:S(2)}) copy-start(s32[4]{0:T(128)} %param.32) | copy-start | bytes 52
  1.7 0.9 %copy-start.11 = (bf16[2,64,512]{2,1,0:T(8,128)(2,1)S(1)}, bf16[2,64,512]{2,1,0:T(8,128)(2,1)}, u32[]{:S(2)}) copy-start(bf16[2,64,512]{2,1,0:T(8,128)(2,1)} %param.31) | copy-start | bytes 393220
  1.7 1.0 %copy-start.12 = (bf16[2,64,512]{2,1,0:T(8,128)(2,1)S(1)}, bf16[2,64,512]{2,1,0:T(8,128)(2,1)}, u32[]{:S(2)}) copy-start(bf16[2,64,512]{2,1,0:T(8,128)(2,1)} %param.30) | copy-start | bytes 393220
  3.1 0.7 %copy-start.13 = (s32[4]{0:T(128)S(1)}, s32[4]{0:T(128)}, u32[]{:S(2)}) copy-start(s32[4]{0:T(128)} %param.34) | copy-start | bytes 52
  3.1 0.7 %copy-start.14 = (s32[4]{0:T(128)S(1)}, s32[4]{0:T(128)}, u32[]{:S(2)}) copy-start(s32[4]{0:T(128)} %param.33) | copy-start | bytes 52
  4.2 2.5 %copy-start.10 = (bf16[2,8,32,128]{3,2,1,0:T(8,128)(2,1)S(1)}, bf16[2,8,32,128]{3,2,1,0:T(8,128)(2,1)}, u32[]{:S(2)}) copy-start(bf16[2,8,32,128]{3,2,1,0:T(8,128)(2,1)} %param.25) | copy-start | bytes 393220
  4.2 16.0 %collective-permute-start.3 = (bf16[2,128,256]{2,1,0:T(8,128)(2,1)S(1)}, bf16[2,128,256]{2,1,0:T(8,128)(2,1)S(1)}, u32[]{:S(2)}, u32[]{:S(2)}) collective-permute-start(bf16[2,128,256]{2,1,0:T(8,128)(2,1)S(1)} %constant_dynamic-slice_fusion), channel_id=1, source_target_pairs={{0,4},{4,8},{8,12},{12,0},{1,5},{5,9},{9,13},{13,1},{2,6},{6,10},{... | collective-permute-start | bytes 393224 | tf_op jit(solution)/shard_map/ppermute | solution.py:90
  4.5 19.2 %collective-permute-start.4 = (bf16[2,128,256]{2,1,0:T(8,128)(2,1)S(1)}, bf16[2,128,256]{2,1,0:T(8,128)(2,1)S(1)}, u32[]{:S(2)}, u32[]{:S(2)}) collective-permute-start(bf16[2,128,256]{2,1,0:T(8,128)(2,1)S(1)} %constant_dynamic-slice_fusion), channel_id=1, source_target_pairs={{0,8},{4,12},{8,0},{12,4},{1,9},{5,13},{9,1},{13,5},{2,10},{6,14},... | collective-permute-start | bytes 393224 | tf_op jit(solution)/shard_map/ppermute | solution.py:90
  6.2 17.5 %collective-permute-start.5 = (bf16[2,128,256]{2,1,0:T(8,128)(2,1)S(1)}, bf16[2,128,256]{2,1,0:T(8,128)(2,1)S(1)}, u32[]{:S(2)}, u32[]{:S(2)}) collective-permute-start(bf16[2,128,256]{2,1,0:T(8,128)(2,1)S(1)} %constant_dynamic-slice_fusion), channel_id=1, source_target_pairs={{0,12},{4,0},{8,4},{12,8},{1,13},{5,1},{9,5},{13,9},{2,14},{6,2},{... | collective-permute-start | bytes 393224 | tf_op jit(solution)/shard_map/ppermute | solution.py:90
  6.6 17.2 %collective-permute-start = (bf16[2,8,32,128]{3,2,1,0:T(8,128)(2,1)S(1)}, bf16[2,8,32,128]{3,2,1,0:T(8,128)(2,1)}, u32[]{:S(2)}, u32[]{:S(2)}) collective-permute-start(bf16[2,8,32,128]{3,2,1,0:T(8,128)(2,1)S(1)} %copy-done.10), channel_id=1, source_target_pairs={{0,4},{4,8},{8,12},{12,0},{1,5},{5,9},{9,13},{13,1},{2,6},{6,10},{... | collective-permute-start | bytes 393224 | tf_op jit(solution)/shard_map/ppermute | solution.py:90
  10.0 19.2 %collective-permute-start.1 = (bf16[2,8,32,128]{3,2,1,0:T(8,128)(2,1)S(1)}, bf16[2,8,32,128]{3,2,1,0:T(8,128)(2,1)}, u32[]{:S(2)}, u32[]{:S(2)}) collective-permute-start(bf16[2,8,32,128]{3,2,1,0:T(8,128)(2,1)S(1)} %copy-done.10), channel_id=1, source_target_pairs={{0,8},{4,12},{8,0},{12,4},{1,9},{5,13},{9,1},{13,5},{2,10},{6,14},... | collective-permute-start | bytes 393224 | tf_op jit(solution)/shard_map/ppermute | solution.py:90
  10.0 2.4 %copy-start.8 = (f32[128,8]{0,1:T(8,128)S(1)}, f32[128,8]{0,1:T(8,128)}, u32[]{:S(2)}) copy-start(f32[128,8]{0,1:T(8,128)} %param.23) | copy-start | bytes 12292
  10.0 2.3 %copy-start.7 = (f32[128,8]{0,1:T(8,128)S(1)}, f32[128,8]{0,1:T(8,128)}, u32[]{:S(2)}) copy-start(f32[128,8]{0,1:T(8,128)} %param.22) | copy-start | bytes 12292
  10.1 3.2 %copy-start.2 = (bf16[128,1024]{1,0:T(8,128)(2,1)S(1)}, bf16[128,1024]{1,0:T(8,128)(2,1)}, u32[]{:S(2)}) copy-start(bf16[128,1024]{1,0:T(8,128)(2,1)} %value_ref.1) | copy-start | bytes 786436
  11.9 1.3 %copy-start.15 = (s32[8]{0:T(128)S(1)}, s32[8]{0:T(128)}, u32[]{:S(2)}) copy-start(s32[8]{0:T(128)} %param.35) | copy-start | bytes 100
  12.0 1.3 %copy-start.5 = (bf16[128,512]{1,0:T(8,128)(2,1)S(1)}, bf16[128,512]{1,0:T(8,128)(2,1)}, u32[]{:S(2)}) copy-start(bf16[128,512]{1,0:T(8,128)(2,1)} %query_ref.2) | copy-start | bytes 393220
  12.0 1.3 %copy-start.6 = (bf16[128,512]{1,0:T(8,128)(2,1)S(1)}, bf16[128,512]{1,0:T(8,128)(2,1)}, u32[]{:S(2)}) copy-start(bf16[128,512]{1,0:T(8,128)(2,1)} %key_ref.1) | copy-start | bytes 393220
  20.3 8.9 %collective-permute-start.2 = (bf16[2,8,32,128]{3,2,1,0:T(8,128)(2,1)S(1)}, bf16[2,8,32,128]{3,2,1,0:T(8,128)(2,1)}, u32[]{:S(2)}, u32[]{:S(2)}) collective-permute-start(bf16[2,8,32,128]{3,2,1,0:T(8,128)(2,1)S(1)} %copy-done.10), channel_id=1, source_target_pairs={{0,12},{4,0},{8,4},{12,8},{1,13},{5,1},{9,5},{13,9},{2,14},{6,2},{... | collective-permute-start | bytes 393224 | tf_op jit(solution)/shard_map/ppermute | solution.py:90
  23.7 29.9 %collective-permute-start.6 = (bf16[3,2,128,256]{3,2,1,0:T(8,128)(2,1)S(1)}, bf16[3,2,128,256]{3,2,1,0:T(8,128)(2,1)S(1)}, u32[]{:S(2)}, u32[]{:S(2)}) collective-permute-start(bf16[3,2,128,256]{3,2,1,0:T(8,128)(2,1)S(1)} %pad_maximum_fusion.1.rest_0_), channel_id=1, source_target_pairs={{0,1},{1,0},{2,3},{3,2},{4,5},{5,4},{6,7},{7,6},{8,9},{9,8},{10,11... | collective-permute-start | bytes 1179656 | tf_op jit(solution)/shard_map/ppermute | solution.py:90
  34.0 16.6 %copy-start.1 = (bf16[128,1024]{1,0:T(8,128)(2,1)S(1)}, bf16[128,1024]{1,0:T(8,128)(2,1)}, u32[]{:S(2)}) copy-start(bf16[128,1024]{1,0:T(8,128)(2,1)} %gate_ref.2) | copy-start | bytes 786436
  50.5 0.7 %copy-start.9 = (f32[128]{0:T(128)S(1)}, f32[128]{0:T(128)}, u32[]{:S(2)}) copy-start(f32[128]{0:T(128)} %param.24) | copy-start | bytes 1540
  51.2 0.9 %copy-start = (bf16[8,128,128]{2,1,0:T(8,128)(2,1)S(1)}, bf16[8,128,128]{2,1,0:T(8,128)(2,1)}, u32[]{:S(2)}) copy-start(bf16[8,128,128]{2,1,0:T(8,128)(2,1)} %shard_map.186.into_ref) | copy-start | bytes 786436
  52.1 1.5 %copy-start.3 = (bf16[128,1024]{1,0:T(8,128)(2,1)S(1)}, bf16[128,1024]{1,0:T(8,128)(2,1)}, u32[]{:S(2)}) copy-start(bf16[128,1024]{1,0:T(8,128)(2,1)} %query_ref.3) | copy-start | bytes 786436
  52.2 1.5 %copy-start.4 = (bf16[128,1024]{1,0:T(8,128)(2,1)S(1)}, bf16[128,1024]{1,0:T(8,128)(2,1)}, u32[]{:S(2)}) copy-start(bf16[128,1024]{1,0:T(8,128)(2,1)} %gate_ref.3) | copy-start | bytes 786436

commit v5 on v4

--- a/solution.py
+++ b/solution.py
@@ -357,8 +357,11 @@
     new_value = lax.dynamic_slice_in_dim(at_value, kv_head * HD, HD, 1)
     cached_key = lax.dynamic_slice_in_dim(prefix_key, kv_head * HD, HD, 2)
     cached_value = lax.dynamic_slice_in_dim(prefix_value, kv_head * HD, HD, 2)
-    states = jnp.stack([prefix_state] + from_others(prefix_state, "context", size, size))
-    states = jnp.take(states, (device - jnp.arange(size, dtype=jnp.int32)) % size, axis=0)
+    turned = from_others(prefix_state, "context", size, size)
+    states = jnp.stack([prefix_state] + turned)
+    states = jnp.take(
+        states, (device - jnp.arange(size, dtype=jnp.int32)) % size, axis=0, mode="clip"
+    )
     states = jnp.moveaxis(states, 0, 2)
     states = states.reshape(states.shape[:2] + (-1, DK))
     slots_here = cached_key.shape[0]
@@ -370,6 +373,7 @@
     share = block_rows // sharers
     share_index = lax.axis_index("head") % sharers
     mine = lax.dynamic_slice_in_dim(own_block, share_index * share, share, 1)
+    mine = lax.optimization_barrier((mine, turned[0]))[0]
     received = jnp.stack(from_others(mine, "context", size, size))
     siblings = from_others(received, "head", lax.axis_size("head"), sharers)
     cached_rows = cached_key.shape[0] * cached_key.shape[1]

time: 57.2 us -> 60.8 us (1.063)
  Pallas kernels: 27.2 us -> 28.9 us
  other arithmetic: 4.49 us -> 5.67 us
    pallas_call x1, Pallas kernels: 16.5 us -> 18.3 us  [chain(): pl.pallas_call(lambda *refs: chain_kernel(size, *refs), out_shape=jax.Sha...]
    select_n x2 -> x1, other arithmetic: 1.17 us -> 0.01 us  [shards(): (device - jnp.arange(size, dtype=jnp.int32)) % size]
    another operation x1, other arithmetic: 0.05 us -> 0.95 us  [shards(): received = jnp.stack(from_others(mine, 'context', size, size))]
    unnamed x39 -> x45, local copies, waits for them, and re-layouts: 3.34 us -> 4.23 us
    gather x1, local copies, waits for them, and re-layouts: 1.4 us -> 0.65 us  [shards(): jnp.take(states, (device - jnp.arange(size, dtype=jnp.int32)) % size, axi...]
    reduce_sum x1, other arithmetic: 0.09 us -> 0.76 us  [row_layout(): offset = jnp.sum(choose * req_offset[None, :], axis=1)]
    sub x1, other arithmetic: 0.01 us -> 0.66 us  [row_layout(): starts = jnp.cumsum(req_len) - req_len]
  transfers between devices with their start and end apart: 7 -> 7, of which waited for: 1 -> 1; matrix products, arithmetic and copies ran while one was open for 15% -> 16% of each run, Pallas kernels for 42% -> 43%
where the time goes in v5:
time: 60.8 us; the launch traced here: 60.4 us
  Pallas kernels  28.9 us (48%)
  local copies, waits for them, and re-layouts  7.99 us (13%)
  starting transfers between devices  7.15 us (12%)
  waiting for transfers between devices  5.9 us (10%)
  other arithmetic  5.67 us (9%)
  between operations  3.78 us (6%)
  matrix products  1.02 us (2%)
    pallas_call x1, Pallas kernels, chain(): pl.pallas_call(lambda *refs: chain_kernel(size, *refs), out_shape=jax.Sha...  18.3 us
    pallas_call x3, Pallas kernels, whole_call(): pl.pallas_call(kernel, out_shape=shapes, in_specs=[space] * len(arrays),...  10.6 us
    ppermute x7, starting transfers between devices, from_others(): lax.ppermute(x, axis, [(i, i // span * span + (i + step) % span) for i in...  7.15 us
    ppermute x7, waiting for transfers between devices, from_others(): lax.ppermute(x, axis, [(i, i // span * span + (i + step) % span) for i in...  5.9 us
    unnamed x45, local copies, waits for them, and re-layouts  4.23 us
  transfers between devices with their start and end apart: 7, of which 1 were waited for; matrix products, arithmetic and copies ran while one was open for 16% of the time, Pallas kernels for 43%

profile of v5, /device:TPU:28, one launch (start us, length us, event | category | flops | bytes accessed | tf_op | source)
XLA Modules:
  0.0 60.4 jit_solution(8869365455798143502)
XLA Ops:
  0.6 0.3 collective-permute-start
  0.9 1.7 %collective-permute-start.1 = (bf16[2,8,32,128]{3,2,1,0:T(8,128)(2,1)}, bf16[2,8,32,128]{3,2,1,0:T(8,128)(2,1)S(1)}, u32[]{:S(2)}, u32[]{:S(2)}) collective-permute-start(bf16[2,8,32,128]{3,2,1,0:T(8,128)(2,1)} %param.25), channel_id=1, source_target_pairs={{0,8},{4,12},{8,0},{12,4},{1,9},{5,13},{9,1},{13,5},{2,10},{6,14},... | collective-permute-start | bytes 393224 | tf_op jit(solution)/shard_map/ppermute | solution.py:90
  2.6 0.4 collective-permute-start.2
  3.2 0.8 %reduce-window.9 = s32[4,1]{0,1:T(1,128)S(1)} reduce-window(s32[4,1]{0,1:T(1,128)} %bitcast.95, s32[]{:T(128)} %constant.131.clone.1), window={size=4x1 pad=3_0x0_0}, to_apply=%region_0.0 | reduce-window | flops 12 | bytes 36 | tf_op jit(solution)/shard_map/reduce-window.4
  4.0 0.7 %bitcast_subtract_fusion = s32[4]{0:T(128)S(1)} fusion(s32[4]{0:T(128)} %param.32, s32[4,1]{0,1:T(1,128)S(1)} %reduce-window.9), kind=kLoop, calls=%fused_computation.101 | loop fusion | flops 4 | bytes 48 | tf_op jit(solution)/shard_map/sub | solution.py:308
  4.7 0.1 convert_reduce_fusion.1
  4.8 0.5 add_bitcast_fusion
  5.3 0.8 %select_reduce_fusion.1 = (s32[128]{0:T(128)S(1)}, s32[128]{0:T(128)S(1)}, s32[128]{0:T(128)S(1)}) fusion(s32[4]{0:T(128)} %param.34, s32[128]{0:T(128)S(1)} %get-tuple-element.30, s32[4]{0:T(128)S(1)} %bitcast_subtract_fusion, s32[4]{0:T(128)} %param.33), kind=kLoop, calls=%fused_computation.71 | loop fusion | flops 3200 | bytes 2096 | tf_op jit(solution)/shard_map/reduce_sum | solution.py:316
  6.0 0.6 fusion.35
  7.4 0.9 %constant_dynamic-slice_fusion.1 = (bf16[128,256]{1,0:T(8,128)(2,1)S(1)}, bf16[128,256]{1,0:T(8,128)(2,1)S(1)}) fusion(bf16[128,512]{1,0:T(8,128)(2,1)S(1)} %copy-done.13, s32[]{:T(128)S(6)} %select_n.167, bf16[128,512]{1,0:T(8,128)(2,1)} %param.28), kind=kLoop, calls=%fused_computation.86 | loop fusion | bytes 262148 | tf_op jit(solution)/shard_map/dynamic_slice | solution.py:357
  8.3 0.1 copy.78
  8.4 0.3 fusion.4
  8.8 0.1 fusion.9
  8.9 0.4 copy-done.14
  9.4 0.1 copy.80
  9.5 0.1 copy.81
  9.6 0.1 copy.84
  9.8 0.1 copy.82
  10.0 0.1 broadcast_bitcast_fusion
  10.1 0.1 convert_reduce_fusion
  10.2 0.1 pad.28.clone
  10.3 0.1 pad.31.clone
  10.4 0.1 copy.73.seg_ref
  10.5 0.2 copy-done.7
  10.7 0.1 copy.71.logit_ref
  10.9 0.1 copy.72.decay_ref
  11.6 0.1 select_reduce_fusion
  11.8 0.7 %copy-done.5 = bf16[128,512]{1,0:T(8,128)(2,1)S(1)} copy-done((bf16[128,512]{1,0:T(8,128)(2,1)S(1)}, bf16[128,512]{1,0:T(8,128)(2,1)}, u32[]{:S(2)}) %copy-start.5) | copy-done | bytes 131096
  12.5 6.0 %shard_map.185 = (f32[8,128,128]{2,1,0:T(8,128)S(1)}, bf16[8,128,128]{2,1,0:T(8,128)(2,1)S(1)}, bf16[8,128,128]{2,1,0:T(8,128)(2,1)S(1)}, f32[8,128,128]{2,1,0:T(8,128)S(1)}) custom-call(bf16[128,512]{1,0:T(8,128)(2,1)S(1)} %copy-done.5, bf16[128,512]{1,0:T(8,128)(2,1)S(1)} %copy-done.6, bf16[128,1024]{1,0:T(8,128)(2,1)S(1)} %copy-done.2, ...), custom_call_target="tpu_custom_call" | custom-call | tf_op jit(solution)/shard_map/pallas_call | solution.py:267
  18.5 0.7 %broadcast_select_fusion.refs_0_ = bf16[8,128,128]{2,1,0:T(8,128)(2,1)} fusion(bf16[8,128,128]{2,1,0:T(8,128)(2,1)S(1)} %get-tuple-element.9, pred[]{:T(512)S(6)} %ge.3), kind=kLoop, calls=%fused_computation.8 | loop fusion | flops 131072 | bytes 524289 | tf_op jit(solution)/shard_map/jit(_where)/select_n | solution.py:406
  19.3 0.1 maximum_maximum_fusion
  19.5 3.4 %collective-permute-start.3 = (bf16[2,128,256]{2,1,0:T(8,128)(2,1)S(1)}, bf16[2,128,256]{2,1,0:T(8,128)(2,1)S(1)}, u32[]{:S(2)}, u32[]{:S(2)}) collective-permute-start(bf16[2,128,256]{2,1,0:T(8,128)(2,1)S(1)} %constant_dynamic-slice_fusion), channel_id=1, source_target_pairs={{0,4},{4,8},{8,12},{12,0},{1,5},{5,9},{9,13},{13,1},{2,6},{6,10},{... | collective-permute-start | bytes 393224 | tf_op jit(solution)/shard_map/ppermute | solution.py:90
  22.9 1.2 %collective-permute-start.5 = (bf16[2,128,256]{2,1,0:T(8,128)(2,1)S(1)}, bf16[2,128,256]{2,1,0:T(8,128)(2,1)}, u32[]{:S(2)}, u32[]{:S(2)}) collective-permute-start(bf16[2,128,256]{2,1,0:T(8,128)(2,1)S(1)} %constant_dynamic-slice_fusion), channel_id=1, source_target_pairs={{0,12},{4,0},{8,4},{12,8},{1,13},{5,1},{9,5},{13,9},{2,14},{6,2},{... | collective-permute-start | bytes 393224 | tf_op jit(solution)/shard_map/ppermute | solution.py:90
  24.2 0.6 slice.31
  24.8 0.1 copy.83.row_ref
  26.2 0.1 copy.76
  26.3 0.1 pad_maximum_fusion
  26.4 0.6 %gather_fusion = bf16[4,2,8,32,128]{4,3,2,1,0:T(8,128)(2,1)S(1)} fusion(bf16[4,2,8,32,128]{4,3,2,1,0:T(8,128)(2,1)S(1)} %pad_maximum_fusion, s32[1024]{0:T(1024)S(1)} %pad_clamp_fusion), kind=kCustom, calls=%fused_computation | custom fusion | bytes 1048592 | tf_op jit(solution)/shard_map/jit(_take)/gather | solution.py:362
  27.1 0.7 %copy-done.10 = bf16[4,2,8,32,128]{4,3,2,1,0:T(8,128)(2,1)} copy-done((bf16[4,2,8,32,128]{4,3,2,1,0:T(8,128)(2,1)}, bf16[4,2,8,32,128]{4,3,2,1,0:T(8,128)(2,1)S(1)}, u32[]{:S(2)}) %copy-start.10) | copy-done | bytes 524312
  27.8 5.9 %collective-permute-done.4 = bf16[2,128,256]{2,1,0:T(8,128)(2,1)S(1)} collective-permute-done((bf16[2,128,256]{2,1,0:T(8,128)(2,1)S(1)}, bf16[2,128,256]{2,1,0:T(8,128)(2,1)S(1)}, u32[]{:S(2)}, u32[]{:S(2)}) %collective-permute-start.4) | collective-permute-done | bytes 131104 | tf_op jit(solution)/shard_map/ppermute | solution.py:90
  33.7 0.9 %pad_maximum_fusion.1.rest_0_ = bf16[3,2,128,256]{3,2,1,0:T(8,128)(2,1)S(1)} fusion(bf16[1,2,128,256]{3,2,1,0:T(8,128)(2,1)} %bitcast.36, bf16[1,2,128,256]{3,2,1,0:T(8,128)(2,1)S(1)} %bitcast.82, bf16[1,2,128,256]{3,2,1,0:T(8,128)(2,1)S(1)} %bitcast.81), kind=kLoop, calls=%fused_computation.4 | loop fusion | flops 393216 | bytes 786432 | tf_op jit(solution)/shard_map/stack | solution.py:377
  34.7 0.1 collective-permute-start.6
  34.8 1.0 %fusion.refs_1_ = f32[8,128,128]{2,1,0:T(8,128)} fusion(f32[8,128,128]{2,1,0:T(8,128)S(1)} %get-tuple-element.10, bf16[8,128,128]{2,1,0:T(8,128)(2,1)S(1)} %bitcast.77, bf16[8,128,128]{2,1,0:T(8,128)(2,1)S(1)} %get-tuple-element.9, pred[]{:T(512)S(6)} %ge.3), kind=kOutput, calls=%fused_computation.2 | convolution fusion | flops 33816576 | bytes 1572865 | tf_op jit(solution)/shard_map/hvj,hjk->hvk/dot_general | solution.py:404
  35.9 18.3 %shard_map.186.into_ref = bf16[8,128,128]{2,1,0:T(8,128)(2,1)} custom-call(bf16[8,128,128]{2,1,0:T(8,128)(2,1)} %broadcast_select_fusion.refs_0_, f32[8,128,128]{2,1,0:T(8,128)} %fusion.refs_1_), custom_call_target="tpu_custom_call" | custom-call | tf_op jit(solution)/shard_map/pallas_call | solution.py:73
  54.2 0.6 %copy-done.9 = f32[128]{0:T(128)S(1)} copy-done((f32[128]{0:T(128)S(1)}, f32[128]{0:T(128)}, u32[]{:S(2)}) %copy-start.9) | copy-done | bytes 536
  54.8 0.9 %copy-done = bf16[8,128,128]{2,1,0:T(8,128)(2,1)S(1)} copy-done((bf16[8,128,128]{2,1,0:T(8,128)(2,1)S(1)}, bf16[8,128,128]{2,1,0:T(8,128)(2,1)}, u32[]{:S(2)}) %copy-start) | copy-done | bytes 262168
  55.8 1.5 %shard_map.187 = bf16[128,1024]{1,0:T(8,128)(2,1)} custom-call(f32[8,128,128]{2,1,0:T(8,128)S(1)} %get-tuple-element.7.local_ref, bf16[8,128,128]{2,1,0:T(8,128)(2,1)S(1)} %get-tuple-element.8.reach_ref, bf16[2,8,128,128]{3,2,1,0:T(8,128)(2,1)S(1)} %bitcast.68, bf16[8,128,128]{2,1,0:T(8,128)(2,1)S(1)} %copy-done, f32[128,3]{1,0:T(8,128)S(1)} %bitcast.71, ...), custom_call_target="tpu_custom_call" | custom-call | tf_op jit(solution)/shard_map/pallas_call | solution.py:267
  57.3 3.1 %shard_map.188 = bf16[128,1024]{1,0:T(8,128)(2,1)} custom-call(bf16[128,1024]{1,0:T(8,128)(2,1)S(1)} %copy-done.3, f32[128,128]{1,0:T(8,128)S(1)} %get-tuple-element.33.cos_ref, f32[128,128]{1,0:T(8,128)S(1)} %get-tuple-element.34.sin_ref, bf16[128,1024]{1,0:T(8,128)(2,1)S(1)} %copy-done.4, s32[128,4]{1,0:T(8,128)S(1)} %copy.83.row_ref, ...), custom_call_target="tpu_custom_call" | custom-call | tf_op jit(solution)/shard_map/pallas_call | solution.py:267
  (75 shorter events, 0.6 us)
Async XLA Ops:
  0.6 6.8 %copy-start.13 = (bf16[128,512]{1,0:T(8,128)(2,1)S(1)}, bf16[128,512]{1,0:T(8,128)(2,1)}, u32[]{:S(2)}) copy-start(bf16[128,512]{1,0:T(8,128)(2,1)} %param.29) | copy-start | bytes 393220
  0.6 18.9 %collective-permute-start = (bf16[2,8,32,128]{3,2,1,0:T(8,128)(2,1)}, bf16[2,8,32,128]{3,2,1,0:T(8,128)(2,1)S(1)}, u32[]{:S(2)}, u32[]{:S(2)}) collective-permute-start(bf16[2,8,32,128]{3,2,1,0:T(8,128)(2,1)} %param.25), channel_id=1, source_target_pairs={{0,4},{4,8},{8,12},{12,0},{1,5},{5,9},{9,13},{13,1},{2,6},{6,10},{... | collective-permute-start | bytes 393224 | tf_op jit(solution)/shard_map/ppermute | solution.py:90
  0.9 25.4 %collective-permute-start.1 = (bf16[2,8,32,128]{3,2,1,0:T(8,128)(2,1)}, bf16[2,8,32,128]{3,2,1,0:T(8,128)(2,1)S(1)}, u32[]{:S(2)}, u32[]{:S(2)}) collective-permute-start(bf16[2,8,32,128]{3,2,1,0:T(8,128)(2,1)} %param.25), channel_id=1, source_target_pairs={{0,8},{4,12},{8,0},{12,4},{1,9},{5,13},{9,1},{13,5},{2,10},{6,14},... | collective-permute-start | bytes 393224 | tf_op jit(solution)/shard_map/ppermute | solution.py:90
  2.6 23.7 %collective-permute-start.2 = (bf16[2,8,32,128]{3,2,1,0:T(8,128)(2,1)}, bf16[2,8,32,128]{3,2,1,0:T(8,128)(2,1)S(1)}, u32[]{:S(2)}, u32[]{:S(2)}) collective-permute-start(bf16[2,8,32,128]{3,2,1,0:T(8,128)(2,1)} %param.25), channel_id=1, source_target_pairs={{0,12},{4,0},{8,4},{12,8},{1,13},{5,1},{9,5},{13,9},{2,14},{6,2},{... | collective-permute-start | bytes 393224 | tf_op jit(solution)/shard_map/ppermute | solution.py:90
  6.0 13.2 %copy-start.17 = (s32[128]{0:T(128)}, s32[128]{0:T(128)S(1)}, u32[]{:S(2)}) copy-start(s32[128]{0:T(128)S(1)} %get-tuple-element.14) | copy-start | bytes 1540
  8.4 0.9 %copy-start.14 = (bf16[2,64,512]{2,1,0:T(8,128)(2,1)S(1)}, bf16[2,64,512]{2,1,0:T(8,128)(2,1)}, u32[]{:S(2)}) copy-start(bf16[2,64,512]{2,1,0:T(8,128)(2,1)} %param.31) | copy-start | bytes 393220
  8.4 1.0 %copy-start.15 = (bf16[2,64,512]{2,1,0:T(8,128)(2,1)S(1)}, bf16[2,64,512]{2,1,0:T(8,128)(2,1)}, u32[]{:S(2)}) copy-start(bf16[2,64,512]{2,1,0:T(8,128)(2,1)} %param.30) | copy-start | bytes 393220
  10.1 0.7 %copy-start.7 = (f32[128,8]{0,1:T(8,128)S(1)}, f32[128,8]{0,1:T(8,128)}, u32[]{:S(2)}) copy-start(f32[128,8]{0,1:T(8,128)} %param.22) | copy-start | bytes 12292
  10.1 1.7 %copy-start.6 = (bf16[128,512]{1,0:T(8,128)(2,1)S(1)}, bf16[128,512]{1,0:T(8,128)(2,1)}, u32[]{:S(2)}) copy-start(bf16[128,512]{1,0:T(8,128)(2,1)} %key_ref.1) | copy-start | bytes 393220
  10.1 0.8 %copy-start.8 = (f32[128,8]{0,1:T(8,128)S(1)}, f32[128,8]{0,1:T(8,128)}, u32[]{:S(2)}) copy-start(f32[128,8]{0,1:T(8,128)} %param.23) | copy-start | bytes 12292
  10.2 1.6 %copy-start.2 = (bf16[128,1024]{1,0:T(8,128)(2,1)S(1)}, bf16[128,1024]{1,0:T(8,128)(2,1)}, u32[]{:S(2)}) copy-start(bf16[128,1024]{1,0:T(8,128)(2,1)} %value_ref.1) | copy-start | bytes 786436
  10.8 0.8 %copy-start.19 = (s32[8]{0:T(128)S(1)}, s32[8]{0:T(128)}, u32[]{:S(2)}) copy-start(s32[8]{0:T(128)} %param.35) | copy-start | bytes 100
  11.6 0.9 %copy-start.5 = (bf16[128,512]{1,0:T(8,128)(2,1)S(1)}, bf16[128,512]{1,0:T(8,128)(2,1)}, u32[]{:S(2)}) copy-start(bf16[128,512]{1,0:T(8,128)(2,1)} %query_ref.2) | copy-start | bytes 393220
  19.2 4.9 %copy-start.16 = (s32[128,1]{0,1:T(1,128)S(1)}, s32[128,1]{0,1:T(1,128)}, u32[]{:S(2)}) copy-start(s32[128,1]{0,1:T(1,128)} %get-tuple-element.27) | copy-start | bytes 1540
  19.3 4.9 %copy-start.18 = (s32[128]{0:T(128)S(1)}, s32[128]{0:T(128)}, u32[]{:S(2)}) copy-start(s32[128]{0:T(128)} %copy-done.17) | copy-start | bytes 1540
  19.4 6.9 %copy-start.12 = (bf16[2,8,32,128]{3,2,1,0:T(8,128)(2,1)S(1)}, bf16[2,8,32,128]{3,2,1,0:T(8,128)(2,1)}, u32[]{:S(2)}) copy-start(bf16[2,8,32,128]{3,2,1,0:T(8,128)(2,1)} %param.25) | copy-start | bytes 393220
  19.5 8.3 %collective-permute-start.3 = (bf16[2,128,256]{2,1,0:T(8,128)(2,1)S(1)}, bf16[2,128,256]{2,1,0:T(8,128)(2,1)S(1)}, u32[]{:S(2)}, u32[]{:S(2)}) collective-permute-start(bf16[2,128,256]{2,1,0:T(8,128)(2,1)S(1)} %constant_dynamic-slice_fusion), channel_id=1, source_target_pairs={{0,4},{4,8},{8,12},{12,0},{1,5},{5,9},{9,13},{13,1},{2,6},{6,10},{... | collective-permute-start | bytes 393224 | tf_op jit(solution)/shard_map/ppermute | solution.py:90
  22.9 10.8 %collective-permute-start.4 = (bf16[2,128,256]{2,1,0:T(8,128)(2,1)S(1)}, bf16[2,128,256]{2,1,0:T(8,128)(2,1)S(1)}, u32[]{:S(2)}, u32[]{:S(2)}) collective-permute-start(bf16[2,128,256]{2,1,0:T(8,128)(2,1)S(1)} %constant_dynamic-slice_fusion), channel_id=1, source_target_pairs={{0,8},{4,12},{8,0},{12,4},{1,9},{5,13},{9,1},{13,5},{2,10},{6,14},... | collective-permute-start | bytes 393224 | tf_op jit(solution)/shard_map/ppermute | solution.py:90
  22.9 10.8 %collective-permute-start.5 = (bf16[2,128,256]{2,1,0:T(8,128)(2,1)S(1)}, bf16[2,128,256]{2,1,0:T(8,128)(2,1)}, u32[]{:S(2)}, u32[]{:S(2)}) collective-permute-start(bf16[2,128,256]{2,1,0:T(8,128)(2,1)S(1)} %constant_dynamic-slice_fusion), channel_id=1, source_target_pairs={{0,12},{4,0},{8,4},{12,8},{1,13},{5,1},{9,5},{13,9},{2,14},{6,2},{... | collective-permute-start | bytes 393224 | tf_op jit(solution)/shard_map/ppermute | solution.py:90
  27.1 0.8 %copy-start.10 = (bf16[4,2,8,32,128]{4,3,2,1,0:T(8,128)(2,1)}, bf16[4,2,8,32,128]{4,3,2,1,0:T(8,128)(2,1)S(1)}, u32[]{:S(2)}) copy-start(bf16[4,2,8,32,128]{4,3,2,1,0:T(8,128)(2,1)S(1)} %gather_fusion) | copy-start | bytes 1572868
  27.8 6.9 %copy-start.11 = (bf16[4,2,8,32,128]{4,3,2,1,0:T(8,128)(2,1)S(1)}, bf16[4,2,8,32,128]{4,3,2,1,0:T(8,128)(2,1)}, u32[]{:S(2)}) copy-start(bf16[4,2,8,32,128]{4,3,2,1,0:T(8,128)(2,1)} %copy-done.10) | copy-start | bytes 1572868
  34.7 22.6 %collective-permute-start.6 = (bf16[3,2,128,256]{3,2,1,0:T(8,128)(2,1)S(1)}, bf16[3,2,128,256]{3,2,1,0:T(8,128)(2,1)S(1)}, u32[]{:S(2)}, u32[]{:S(2)}) collective-permute-start(bf16[3,2,128,256]{3,2,1,0:T(8,128)(2,1)S(1)} %pad_maximum_fusion.1.rest_0_), channel_id=1, source_target_pairs={{0,1},{1,0},{2,3},{3,2},{4,5},{5,4},{6,7},{7,6},{8,9},{9,8},{10,11... | collective-permute-start | bytes 1179656 | tf_op jit(solution)/shard_map/ppermute | solution.py:90
  35.9 18.3 %copy-start.1 = (bf16[128,1024]{1,0:T(8,128)(2,1)S(1)}, bf16[128,1024]{1,0:T(8,128)(2,1)}, u32[]{:S(2)}) copy-start(bf16[128,1024]{1,0:T(8,128)(2,1)} %gate_ref.2) | copy-start | bytes 786436
  54.2 0.7 %copy-start.9 = (f32[128]{0:T(128)S(1)}, f32[128]{0:T(128)}, u32[]{:S(2)}) copy-start(f32[128]{0:T(128)} %param.24) | copy-start | bytes 1540
  54.8 0.9 %copy-start = (bf16[8,128,128]{2,1,0:T(8,128)(2,1)S(1)}, bf16[8,128,128]{2,1,0:T(8,128)(2,1)}, u32[]{:S(2)}) copy-start(bf16[8,128,128]{2,1,0:T(8,128)(2,1)} %shard_map.186.into_ref) | copy-start | bytes 786436
  55.8 1.5 %copy-start.3 = (bf16[128,1024]{1,0:T(8,128)(2,1)S(1)}, bf16[128,1024]{1,0:T(8,128)(2,1)}, u32[]{:S(2)}) copy-start(bf16[128,1024]{1,0:T(8,128)(2,1)} %query_ref.3) | copy-start | bytes 786436
  55.8 1.5 %copy-start.4 = (bf16[128,1024]{1,0:T(8,128)(2,1)S(1)}, bf16[128,1024]{1,0:T(8,128)(2,1)}, u32[]{:S(2)}) copy-start(bf16[128,1024]{1,0:T(8,128)(2,1)} %gate_ref.3) | copy-start | bytes 786436
